TPU v7x, 32 devices: a whole 2x2x4 slice. The times are simulated.
32 devices in a mesh: batch: 8 (over z, x), seq: 4 (over y, core).
Axes of the slice: x: 2, y: 2, z: 4, core: 2. Of those that a mesh axis runs over, the one named last changes fastest.
Arguments:
- hidden: bfloat16 [8, 2048, 1536], P('batch', 'seq'), may hold values from -6 to 6
- in_proj: bfloat16 [1536, 6448], P(('batch', 'seq')), may hold values from -1 to 1
- out_proj: bfloat16 [3072, 1536], P(('batch', 'seq')), may hold values from -0.109375 to 0.109375
- conv_weight: bfloat16 [4, 3328], P(None, ('batch', 'seq')), may hold values from -3 to 3
- conv_bias: bfloat16 [3328], P(('batch', 'seq')), may hold values from -1.5 to 1.5
- step_bias: float32 [48], replicated, may hold values from -10 to -3
- decay_log: float32 [48], replicated, may hold values from -1.2 to 0.7
- skip_weight: float32 [48], replicated, may hold values from 0.2 to 1.5
- gated_gain: bfloat16 [3072], P(('batch', 'seq')), may hold values from 0.5 to 1.5
- norm_gain: bfloat16 [1536], P(('batch', 'seq')), may hold values from 0.5 to 1.5
- cotangent: bfloat16 [8, 2048, 1536], P('batch', 'seq'), may hold values from -6 to 6
Outputs:
- output: bfloat16 [8, 2048, 1536], P('batch', 'seq')
- hidden_grad: bfloat16 [8, 2048, 1536], P('batch', 'seq')
- in_proj_grad: float32 [1536, 6448], P(('batch', 'seq'))
- out_proj_grad: float32 [3072, 1536], P(('batch', 'seq'))
- conv_weight_grad: float32 [4, 3328], P(None, ('batch', 'seq'))
- conv_bias_grad: float32 [3328], P(('batch', 'seq'))
- step_bias_grad: float32 [48], replicated
- decay_log_grad: float32 [48], replicated
- skip_weight_grad: float32 [48], replicated
- gated_gain_grad: float32 [3072], P(('batch', 'seq'))
- norm_gain_grad: float32 [1536], P(('batch', 'seq'))
All inputs are finite; a program needn't handle non-finite values.
Results may differ from a plain program's by a relative error of at most 0.0096.
Values may be sent and summed in bfloat16 or wider, within the bound.
No kernel may reach another device: no remote copies, remote signals or barrier semaphores. Data moves between devices by JAX's collectives and lax.ppermute only.
A program may use at most 320 MiB of HBM per device.

v0:
```python
import jax
import jax.numpy as jnp
from jax import lax
from jax.sharding import PartitionSpec as P

HEAD_COUNT = 48
P_SIZE = 64
NS = 128
KCONV = 4
BLOCK = 256
DI = 3072
CONV_CH = 3328


EPSILON = 1e-05
HIGHEST = lax.Precision.HIGHEST


def shifted(value, axis, steps):
    count = lax.axis_size(axis)
    initial, last = (max(0, -steps), min(count, count - steps))
    return lax.ppermute(value, axis, [(source, source + steps) for source in range(initial, last)])


def carried_in(value, axis, combine, identity):
    count, here = (lax.axis_size(axis), lax.axis_index(axis))
    everything = jax.tree.map(lambda part: lax.all_gather(part, axis), value)
    start = jax.tree.map(
        lambda part, zero: jnp.broadcast_to(jnp.asarray(zero, part.dtype), part.shape),
        value,
        identity,
    )

    def step(k, before):
        reached = k < here
        new = combine(before, jax.tree.map(lambda part: part[k], everything))
        return jax.tree.map(lambda a, b: jnp.where(reached, a, b), new, before)

    return lax.fori_loop(0, count, step, start)


def prefix(value, axis, join, neutral):
    count = lax.axis_size(axis)
    place = lax.axis_index(axis)
    ahead = count - 1 - place
    gathered = jax.tree.map(
        lambda a, kind: lax.all_gather(a.astype(kind), axis),
        value,
        jax.tree.map(lambda a: jnp.bfloat16 if a.dtype == jnp.float32 else a.dtype, value),
    )
    state = jax.tree.map(lambda a, e: jnp.zeros_like(a) + jnp.asarray(e, a.dtype), value, neutral)

    def one(step, state):
        source = count - 1 - step
        return join(
            state,
            jax.tree.map(
                lambda a, own: lax.dynamic_index_in_dim(a, source, 0, False).astype(own.dtype),
                gathered,
                value,
            ),
        )

    return lax.fori_loop(0, ahead, one, state)


def for_sending(value):

    def short(part):
        return part.astype(jnp.bfloat16) if part.dtype == jnp.float32 else part

    return jax.tree.map(short, value)


def prenorm(stream, norm_scale):
    return (
        stream * lax.rsqrt(jnp.mean(stream * stream, axis=-1, keepdims=True) + EPSILON) * norm_scale
    )


def block_terms(pieces):
    x_part, write_part, read_part, decay_part = pieces
    within = jnp.cumsum(decay_part, axis=0)
    across = within.T
    causal = jnp.arange(BLOCK)[:, None] >= jnp.arange(BLOCK)[None, :]
    weights = jnp.exp(jnp.where(causal[None], across[:, :, None] - across[:, None, :], -jnp.inf))
    scores = jnp.dot(read_part, write_part.T, precision=HIGHEST)
    y_inside = jnp.einsum("hts,shp->thp", weights * scores[None], x_part, precision=HIGHEST)
    to_end = jnp.exp(within[-1:] - within)
    state = jnp.einsum("sh,shp,sn->hpn", to_end, x_part, write_part, precision=HIGHEST)
    return (y_inside, state, within)


def local_states(head_inputs, write_map, read_map, step_size, log_decay):
    seq_count = head_inputs.shape[0]
    piece_rows = head_inputs.shape[1]
    per_piece = piece_rows // BLOCK
    block_count = seq_count * per_piece
    scaled_x = (head_inputs * step_size[..., None]).reshape(block_count, BLOCK, HEAD_COUNT, P_SIZE)
    write_blocks = write_map.reshape(block_count, BLOCK, NS)
    read_blocks = read_map.reshape(block_count, BLOCK, NS)
    decay_blocks = log_decay.reshape(block_count, BLOCK, HEAD_COUNT)
    y_inside, states, within = lax.map(
        jax.checkpoint(block_terms), (scaled_x, write_blocks, read_blocks, decay_blocks)
    )
    states = states.reshape(seq_count, per_piece, HEAD_COUNT, P_SIZE, NS)
    block_ends = within[:, -1, :].reshape(seq_count, per_piece, HEAD_COUNT)
    running = jnp.zeros((seq_count, HEAD_COUNT, P_SIZE, NS), jnp.float32)
    entering = []
    for number in range(per_piece):
        entering.append(running)
        running = jnp.exp(block_ends[:, number])[:, :, None, None] * running + states[:, number]
    entering = jnp.stack(entering, axis=1).reshape(block_count, HEAD_COUNT, P_SIZE, NS)
    y_carried = jnp.exp(within)[..., None] * jnp.einsum(
        "ctn,chpn->cthp", read_blocks, entering, precision=HIGHEST
    )
    before = jnp.cumsum(block_ends, axis=1) - block_ends
    device_cum = within.reshape(seq_count, per_piece, BLOCK, HEAD_COUNT) + before[:, :, None, :]
    y_local = (y_inside + y_carried).reshape(seq_count, piece_rows, HEAD_COUNT, P_SIZE)
    return (
        y_local,
        running,
        jnp.sum(block_ends, axis=1),
        device_cum.reshape(seq_count, piece_rows, HEAD_COUNT),
    )


def section_one(extended, raw_step, conv_kernel, conv_offset, step_bias, decay_log):
    piece_rows = raw_step.shape[1]
    seq_count = raw_step.shape[0]
    convolved = conv_offset + conv_kernel[0] * extended[:, 0:piece_rows]
    for offset in range(1, KCONV):
        convolved = convolved + conv_kernel[offset] * extended[:, offset : offset + piece_rows]
    active = jax.nn.silu(convolved)
    head_inputs = active[..., :DI].reshape(seq_count, piece_rows, HEAD_COUNT, P_SIZE)
    write_map = active[..., DI : DI + NS]
    read_map = active[..., DI + NS :]
    step_size = jax.nn.softplus(raw_step + step_bias)
    log_decay = -jnp.exp(decay_log) * step_size
    y_local, final_state, total_decay, device_cum = local_states(
        head_inputs, write_map, read_map, step_size, log_decay
    )
    return (y_local, final_state, total_decay, read_map, device_cum, head_inputs)


def section_two(
    read_map, device_cum, entering, y_local, head_inputs, gate_part, skip_weight, gated_scale
):
    seq_count = y_local.shape[0]
    piece_rows = y_local.shape[1]
    carried = jnp.exp(device_cum)[..., None] * jnp.einsum(
        "stn,shpn->sthp", read_map, entering, precision=HIGHEST
    )
    mixed_y = y_local + carried + skip_weight[None, None, :, None] * head_inputs
    gated_v = mixed_y.reshape(seq_count * piece_rows, DI) * jax.nn.silu(gate_part)
    return (
        gated_v
        * lax.rsqrt(jnp.mean(gated_v * gated_v, axis=-1, keepdims=True) + EPSILON)
        * gated_scale
    )


def combine(earlier_part, later_part):
    return (
        earlier_part[0] + later_part[0],
        jnp.exp(later_part[0])[..., None, None] * earlier_part[1] + later_part[1],
    )


def per_device(
    hidden,
    in_proj,
    out_proj,
    conv_weight,
    conv_bias,
    step_bias,
    decay_log,
    skip_weight,
    gated_gain,
    norm_gain,
    cotangent,
):
    seq_count = hidden.shape[0]
    piece_rows = hidden.shape[1]
    model_width = hidden.shape[2]
    row_count = seq_count * piece_rows
    weight_in, weight_out, kernel_full, offset_full, gated_full, norm_full = (
        lax.all_gather(in_proj, ("batch", "seq"), axis=0, tiled=True),
        lax.all_gather(out_proj, ("batch", "seq"), axis=0, tiled=True),
        lax.all_gather(conv_weight, ("batch", "seq"), axis=1, tiled=True),
        lax.all_gather(conv_bias, ("batch", "seq"), axis=0, tiled=True),
        lax.all_gather(gated_gain, ("batch", "seq"), axis=0, tiled=True),
        lax.all_gather(norm_gain, ("batch", "seq"), axis=0, tiled=True),
    )
    stream = hidden.reshape(row_count, model_width).astype(jnp.float32)
    normed, norm_pull = jax.vjp(prenorm, stream, norm_full.astype(jnp.float32))
    normed_low = normed.astype(jnp.bfloat16)
    projected = jnp.dot(normed_low, weight_in, preferred_element_type=jnp.float32)
    gate_part = projected[:, :DI]
    conv_part = projected[:, DI : DI + CONV_CH].reshape(seq_count, piece_rows, CONV_CH)
    raw_step = projected[:, DI + CONV_CH :].reshape(seq_count, piece_rows, HEAD_COUNT)
    edge_rows = shifted(
        conv_part[:, piece_rows - (KCONV - 1) :].astype(jnp.bfloat16), "seq", 1
    ).astype(jnp.float32)
    extended = jnp.concatenate([edge_rows, conv_part], axis=1)
    conv_kernel = kernel_full.astype(jnp.float32)
    conv_offset = offset_full.astype(jnp.float32)
    y_local, final_state, total_decay, read_map, device_cum, head_inputs = section_one(
        extended, raw_step, conv_kernel, conv_offset, step_bias, decay_log
    )
    prior_decay, entering = carried_in(
        (total_decay, final_state),
        "seq",
        combine,
        (jnp.zeros_like(total_decay), jnp.zeros_like(final_state)),
    )
    gated_scale = gated_full.astype(jnp.float32)
    gated_out = section_two(
        read_map, device_cum, entering, y_local, head_inputs, gate_part, skip_weight, gated_scale
    )
    gated_low = gated_out.astype(jnp.bfloat16)
    result = (stream + jnp.dot(gated_low, weight_out, preferred_element_type=jnp.float32)).astype(
        jnp.bfloat16
    )
    weight_in_back, weight_out_back = (
        lax.all_gather(in_proj, ("batch", "seq"), axis=0, tiled=True),
        lax.all_gather(out_proj, ("batch", "seq"), axis=0, tiled=True),
    )
    upstream = cotangent.reshape(row_count, model_width)
    grad_gated = jnp.einsum(
        "td,kd->tk", upstream, weight_out_back, preferred_element_type=jnp.float32
    )
    grad_out_w = jnp.einsum("tk,td->kd", gated_low, upstream, preferred_element_type=jnp.float32)
    _, second_pull = jax.vjp(
        section_two,
        read_map,
        device_cum,
        entering,
        y_local,
        head_inputs,
        gate_part,
        skip_weight,
        gated_scale,
    )
    (
        grad_read,
        grad_cum,
        grad_enter,
        grad_local,
        grad_heads,
        grad_gate,
        grad_skip,
        grad_gated_scale,
    ) = second_pull(grad_gated)
    later_decay, grad_final = prefix(
        (total_decay, grad_enter),
        "seq",
        combine,
        (jnp.zeros_like(total_decay), jnp.zeros_like(grad_enter)),
    )
    grad_total = jnp.exp(total_decay) * jnp.sum(grad_final * entering, axis=(-2, -1))
    _, first_pull = jax.vjp(
        section_one, extended, raw_step, conv_kernel, conv_offset, step_bias, decay_log
    )
    grad_extended, grad_raw, grad_kernel, grad_offset, grad_bias, grad_rate = first_pull(
        (grad_local, grad_final, grad_total, grad_read, grad_cum, grad_heads)
    )
    edge_back = shifted(for_sending(grad_extended[:, : KCONV - 1]), "seq", -1)
    grad_conv = grad_extended[:, KCONV - 1 :] + jnp.pad(
        edge_back, ((0, 0), (piece_rows - (KCONV - 1), 0), (0, 0))
    )
    grad_proj_low = jnp.concatenate(
        [grad_gate, grad_conv.reshape(row_count, CONV_CH), grad_raw.reshape(row_count, HEAD_COUNT)],
        axis=1,
    ).astype(jnp.bfloat16)
    grad_in_w = jnp.einsum(
        "td,tk->dk", normed_low, grad_proj_low, preferred_element_type=jnp.float32
    )
    grad_normed = jnp.einsum(
        "tk,dk->td", grad_proj_low, weight_in_back, preferred_element_type=jnp.float32
    )
    grad_stream, grad_norm_scale = norm_pull(grad_normed)
    hidden_grad = (upstream.astype(jnp.float32) + grad_stream).astype(jnp.bfloat16)
    (
        in_proj_grad,
        out_proj_grad,
        conv_weight_grad,
        conv_bias_grad,
        gated_gain_grad,
        norm_gain_grad,
    ) = (
        lax.psum_scatter(grad_in_w, ("batch", "seq"), scatter_dimension=0, tiled=True),
        lax.psum_scatter(grad_out_w, ("batch", "seq"), scatter_dimension=0, tiled=True),
        lax.psum_scatter(grad_kernel, ("batch", "seq"), scatter_dimension=1, tiled=True),
        lax.psum_scatter(grad_offset, ("batch", "seq"), scatter_dimension=0, tiled=True),
        lax.psum_scatter(grad_gated_scale, ("batch", "seq"), scatter_dimension=0, tiled=True),
        lax.psum_scatter(grad_norm_scale, ("batch", "seq"), scatter_dimension=0, tiled=True),
    )
    step_bias_grad, decay_log_grad, skip_weight_grad = lax.psum(
        (grad_bias, grad_rate, grad_skip), ("batch", "seq")
    )
    return (
        result.reshape(hidden.shape),
        hidden_grad.reshape(hidden.shape),
        in_proj_grad,
        out_proj_grad,
        conv_weight_grad,
        conv_bias_grad,
        step_bias_grad,
        decay_log_grad,
        skip_weight_grad,
        gated_gain_grad,
        norm_gain_grad,
    )


def solution(mesh):
    in_specs = (
        P("batch", "seq", None),
        P(("batch", "seq"), None),
        P(("batch", "seq"), None),
        P(None, ("batch", "seq")),
        P(("batch", "seq")),
        P(),
        P(),
        P(),
        P(("batch", "seq")),
        P(("batch", "seq")),
        P("batch", "seq", None),
    )
    out_specs = (
        P("batch", "seq", None),
        P("batch", "seq", None),
        P(("batch", "seq"), None),
        P(("batch", "seq"), None),
        P(None, ("batch", "seq")),
        P(("batch", "seq")),
        P(),
        P(),
        P(),
        P(("batch", "seq")),
        P(("batch", "seq")),
    )
    return jax.shard_map(
        per_device, mesh=mesh, in_specs=in_specs, out_specs=out_specs, check_vma=False
    )
```

profile of v0, /device:TPU:0, one launch (start us, length us, event | category | flops | bytes accessed | tf_op | source)
XLA Modules:
  0.0 1654.3 jit_solution(11534178219992642412)
XLA Ops:
  10.5 43.7 %all-reduce.30 = (bf16[1536]{0:T(1024)(128)(2,1)S(1)}, bf16[3328]{0:T(1024)(128)(2,1)S(1)}, bf16[3072]{0:T(1024)(128)(2,1)S(1)}) all-reduce(bf16[1536]{0:T(1024)(128)(2,1)S(1)} %dynamic-update-slice.1, bf16[3328]{0:T(1024)(128)(2,1)S(1)} %dynamic-update-slice, ...), channel_id=1, replica_groups=mesh['batch'=8,'seq'=4] {'batch','seq'}, use_global_device_ids=true, to_apply=%add.21 | all-reduce | flops 7936 | bytes 31744
  54.3 42.0 %all-gather.3 = bf16[32,104,4]{1,2,0:T(4,128)(2,1)S(1)} all-gather(bf16[1,104,4]{1,2,0:T(4,128)(2,1)} %bitcast.579), channel_id=1, replica_groups=mesh['batch'=8,'seq'=4] {'batch','seq'}, dimensions={0}, use_global_device_ids=true | all-gather | bytes 27456 | tf_op jit(solution)/shard_map/all_gather | solution.py:190
  99.1 45.5 %all-gather.9.cloned.1.call-done = bf16[1536,6448]{1,0:T(8,128)(2,1)} async-done(((bf16[48,6448]{1,0:T(8,128)(2,1)}), bf16[1536,6448]{1,0:T(8,128)(2,1)}) %all-gather.9.cloned.1.call-update) | async-done | bytes 19808272 | tf_op jit(solution)/shard_map/all_gather | solution.py:188
  144.6 18.1 %fusion.149 = f32[512,6448]{0,1:T(8,128)} fusion(bf16[1536,6448]{1,0:T(8,128)(2,1)} %all-gather.9.cloned.1.call-done, bf16[1,512,1536]{2,1,0:T(8,128)(2,1)} %param.21, f32[1536]{0:T(1024)S(1)} %convert_element_type.96, f32[512]{0:T(512)S(1)} %fusion.159), kind=kOutput, calls=%fused_computation.226 | convolution fusion | flops 10144972800 | bytes 34594816 | tf_op jit(solution)/shard_map/dot_general | solution.py:198
  174.3 18.9 %fusion.75 = (f32[1,512,3328]{1,2,0:T(8,128)S(1)}, f32[1,512,3328]{1,2,0:T(8,128)}) fusion(f32[512,6448]{0,1:T(8,128)} %fusion.149, f32[3328]{0:T(1024)S(1)} %get-tuple-element.745, f32[1,512,3328]{1,2,0:T(8,128)} %copy-done.5, f32[1,3,3328]{1,2,0:T(8,128)S(1)} %copy.258, f32[3328]{0:T(1024)S(1)} %get-tuple-element.746, f32[3328]{0:T(1024)S(1)} %get-tuple-element.747, ...), kind=kLoop, calls=%fused_computation.134 | loop fusion | flops 25559040 | bytes 27369472 | tf_op jit(solution)/shard_map/jit(silu)/mul | solution.py:134
  214.8 49.4 %while.74 = (s32[]{:T(128)}, f32[2,256,48,64]{1,3,2,0:T(8,128)}, f32[2,48,64,128]{3,2,1,0:T(8,128)S(1)}, f32[2,256,48]{1,2,0:T(8,128)}, f32[2,256,48,64]{1,3,2,0...) while((s32[]{:T(128)}, f32[2,256,48,64]{1,3,2,0:T(8,128)}, ...), condition=%wide.region_4.5_spmd, body=%wide.region_1.4_spmd.sunk | while | flops 3736441088 | bytes 12754685 | solution.py:103
  223.4 16.2 bitcast_dynamic-update-slice_fusion.8
  248.1 16.1 bitcast_dynamic-update-slice_fusion.8
  300.9 12.7 all-gather.11.cloned.1.call-done
  328.9 12.2 multiply_add_fusion
  349.0 49.0 %all-gather.13.cloned.1.call-done = bf16[3072,1536]{1,0:T(8,128)(2,1)} async-done(((bf16[96,1536]{1,0:T(8,128)(2,1)}), bf16[3072,1536]{1,0:T(8,128)(2,1)}) %all-gather.13.cloned.1.call-update) | async-done | bytes 9437200 | tf_op jit(solution)/shard_map/all_gather | solution.py:189
  397.9 11.4 multiply_reduce_fusion.7
  432.7 16.1 while.75
  475.0 10.2 fusion.114
  518.3 291.5 %while.77 = (s32[]{:T(128)}, f32[2,256,48,64]{1,0,3,2:T(2,128)}, f32[2,256,128]{2,1,0:T(8,128)}, f32[2,256,128]{2,1,0:T(8,128)}, f32[2,256,48]{1,0,2:T(2,128)}, ...) while((s32[]{:T(128)}, f32[2,256,48,64]{1,0,3,2:T(2,128)}, ...), condition=%wide.region_33.34_spmd, body=%wide.region_24.33_spmd.sunk | while | flops 7594704896 | bytes 86663040 | solution.py:103
  556.0 19.5 %fusion.255 = (f32[48,256]{1,0:T(8,128)}, f32[48,256]{1,0:T(8,128)}, f32[256,256]{1,0:T(8,128)S(1)}) fusion(f32[256,256]{1,0:T(8,128)S(1)} %fusion.251, f32[48,256]{1,0:T(8,128)S(1)} %get-tuple-element.1134, pred[256,256]{1,0:T(8,128)(4,1)} %iota_compare_fusion.5, f32[256,48,64]{0,2,1:T(8,128)S(1)} %get-tuple-element.1128, ...), kind=kOutput, calls=%fused_computation.67.clone.1 | convolution fusion | flops 2444140544 | bytes 7028736 | tf_op jit(solution)/shard_map/transpose(jvp())/while/body/eval_jaxpr/checkpoint/hts,shp->thp/dot_general | solution.py:88
  584.4 10.6 fusion.253
  607.0 63.3 %dynamic_update_slice.78 = f32[2,256,48,64]{1,0,3,2:T(2,128)} dynamic-update-slice(f32[2,256,48,64]{1,0,3,2:T(2,128)} %get-tuple-element.1267, f32[1,256,48,64]{1,0,3,2:T(1,128)S(1)} %copy.453, s32[]{:T(128)S(6)} %sub.244, s32[]{:T(128)} %constant.201.clone.1..sunk.1, s32[]{:T(128)} %constant.201.clone.1..sunk.1, s32[]{:T(128)} %constant.201.clone.1..sunk.1) | dynamic-update-slice | bytes 6291460 | tf_op jit(solution)/shard_map/transpose(jvp())/while/body/jit(dynamic_update_index_in_dim)/dynamic_update_slice | solution.py:103
  687.7 19.5 %fusion.255 = (f32[48,256]{1,0:T(8,128)}, f32[48,256]{1,0:T(8,128)}, f32[256,256]{1,0:T(8,128)S(1)}) fusion(f32[256,256]{1,0:T(8,128)S(1)} %fusion.251, f32[48,256]{1,0:T(8,128)S(1)} %get-tuple-element.1134, pred[256,256]{1,0:T(8,128)(4,1)} %iota_compare_fusion.5, f32[256,48,64]{0,2,1:T(8,128)S(1)} %get-tuple-element.1128, ...), kind=kOutput, calls=%fused_computation.67.clone.1 | convolution fusion | flops 2444140544 | bytes 7028736 | tf_op jit(solution)/shard_map/transpose(jvp())/while/body/eval_jaxpr/checkpoint/hts,shp->thp/dot_general | solution.py:88
  716.1 10.7 fusion.253
  738.7 63.3 %dynamic_update_slice.78 = f32[2,256,48,64]{1,0,3,2:T(2,128)} dynamic-update-slice(f32[2,256,48,64]{1,0,3,2:T(2,128)} %get-tuple-element.1267, f32[1,256,48,64]{1,0,3,2:T(1,128)S(1)} %copy.453, s32[]{:T(128)S(6)} %sub.244, s32[]{:T(128)} %constant.201.clone.1..sunk.1, s32[]{:T(128)} %constant.201.clone.1..sunk.1, s32[]{:T(128)} %constant.201.clone.1..sunk.1) | dynamic-update-slice | bytes 6291460 | tf_op jit(solution)/shard_map/transpose(jvp())/while/body/jit(dynamic_update_index_in_dim)/dynamic_update_slice | solution.py:103
  809.9 12.9 fusion.137
  847.4 25.1 %multiply_reduce_fusion.5 = (f32[3328]{0:T(1024)S(1)}, f32[3328]{0:T(1024)S(1)}, f32[3328]{0:T(1024)S(1)}, f32[3328]{0:T(1024)}, f32[3328]{0:T(1024)S(1)}, /*index=5*/f32[1,512,3328]{1,2,0:T(8,128)S(1)}) fusion(f32[1,512,3328]{1,2,0:T(8,128)} %copy-done.5, f32[1,3,3328]{1,2,0:T(8,128)} %copy-done.13, f32[512,6448]{0,1:T(8,128)} %fusion.149, ...), kind=kLoop, calls=%fused_computation.131 | loop fusion | flops 39173888 | bytes 34185216 | tf_op jit(solution)/shard_map/transpose(jvp())/reduce_sum | solution.py:133
  872.6 9.8 broadcast_multiply_fusion
  882.4 12.2 pad_add_fusion
  915.0 19.4 %fusion.90 = (f32[1536]{0:T(1024)}, f32[512]{0:T(512)S(1)}, f32[512,1536]{1,0:T(8,128)}) fusion(bf16[1,512,1536]{2,1,0:T(8,128)(2,1)S(1)} %copy-done.19, f32[512]{0:T(512)S(1)} %copy-done.57, f32[1536]{0:T(1024)S(1)} %copy-done.51, bf16[1536,6448]{1,0:T(8,128)(2,1)} %all-gather.9.cloned.1.call-done, bf16[512,48]{0,1:T(8,128)(2,1)S(1)} %get-tuple-element.835, ...), kind=kOutput, calls=%fused_computation.177 | convolution fusion | flops 10167138304 | bytes 31145984 | tf_op jit(solution)/shard_map/tk,dk->td/dot_general | solution.py:279
  934.5 12.2 fusion.121
  946.9 22.3 %fusion.108 = f32[1536,6448]{1,0:T(8,128)} fusion(bf16[512,48]{0,1:T(8,128)(2,1)S(1)} %get-tuple-element.835, bf16[512,3328]{0,1:T(8,128)(2,1)} %copy-done.22, bf16[512,3072]{0,1:T(8,128)(2,1)} %get-tuple-element.857, bf16[1,512,1536]{2,1,0:T(8,128)(2,1)S(1)} %copy-done.19, f32[1536]{0:T(1024)S(1)} %copy-done.51, f32[512]{0:T(512)S(1)} %copy-done.57), kind=kOutput, calls=%fused_computation.196 | convolution fusion | flops 10164781056 | bytes 47800320 | tf_op jit(solution)/shard_map/td,tk->dk/dot_general | solution.py:276
  969.2 11.1 fusion.107
  982.5 77.0 %all-reduce.33.cloned.1.call-done = (f32[4,3328]{1,0:T(4,128)}, f32[3328]{0:T(1024)}, f32[48]{0:T(128)}, f32[48]{0:T(128)}, f32[48]{0:T(128)}, /*index=5*/f32[3072]{0:T(1024)}, f32[1536]{0:T(1024)}) async-done(((f32[4,3328]{1,0:T(4,128)}, f32[3328]{0:T(1024)}, f32[48]{0:T(128)}, f32[48]{0:T(128)}, f32[48]{0:T(128)}, /*index=5*/f32[3072]{0:T(1024)}, f32[1536]{0:T(1024)}), (f32[4,3328]{1,0:T(4,128)}, ...) | async-done | bytes 85584
  1064.7 209.5 %reduce-scatter.6.cloned.1.call-done = f32[96,1536]{1,0:T(8,128)} async-done(((f32[3072,1536]{1,0:T(8,128)}), f32[96,1536]{1,0:T(8,128)}) %reduce-scatter.6.cloned.1.call-update) | async-done | bytes 589840 | tf_op jit(solution)/shard_map/reduce_scatter | solution.py:293
  1274.2 369.7 %reduce-scatter.4.cloned.1.call-done = f32[48,6448]{1,0:T(8,128)} async-done(((f32[1536,6448]{1,0:T(8,128)}), f32[48,6448]{1,0:T(8,128)}) %reduce-scatter.4.cloned.1.call-update) | async-done | bytes 1238032 | tf_op jit(solution)/shard_map/reduce_scatter | solution.py:292
  (422 shorter events, 358.8 us)
Async XLA Ops:
  7.2 137.4 %all-gather.9.cloned.1.call-start = ((), (), s32[]{:S(2)}) async-start(), calls=%async_computation.2 | async-start | bytes 20680704 | tf_op jit(solution)/shard_map/all_gather | solution.py:188
  7.9 305.7 %all-gather.11.cloned.1.call-start = ((), (), s32[]{:S(2)}) async-start(), calls=%async_computation.3 | async-start | bytes 7864320 | tf_op jit(solution)/shard_map/all_gather | solution.py:27
  54.3 108.5 %copy-start.50 = (f32[1536]{0:T(1024)}, f32[1536]{0:T(1024)S(1)}, u32[]{:S(2)}) copy-start(f32[1536]{0:T(1024)S(1)} %convert_element_type.96) | copy-start | bytes 18436
  96.6 77.6 %copy-start.39 = (f32[3328]{0:T(1024)}, f32[3328]{0:T(1024)S(1)}, u32[]{:S(2)}) copy-start(f32[3328]{0:T(1024)S(1)} %get-tuple-element.744) | copy-start | bytes 39940
  96.6 77.6 %copy-start.41 = (f32[3328]{0:T(1024)}, f32[3328]{0:T(1024)S(1)}, u32[]{:S(2)}) copy-start(f32[3328]{0:T(1024)S(1)} %get-tuple-element.745) | copy-start | bytes 39940
  96.6 77.6 %copy-start.43 = (f32[3328]{0:T(1024)}, f32[3328]{0:T(1024)S(1)}, u32[]{:S(2)}) copy-start(f32[3328]{0:T(1024)S(1)} %get-tuple-element.746) | copy-start | bytes 39940
  96.6 77.6 %copy-start.45 = (f32[3328]{0:T(1024)}, f32[3328]{0:T(1024)S(1)}, u32[]{:S(2)}) copy-start(f32[3328]{0:T(1024)S(1)} %get-tuple-element.747) | copy-start | bytes 39940
  98.4 64.3 %copy-start.52 = (f32[512]{0:T(512)}, f32[512]{0:T(512)S(1)}, u32[]{:S(2)}) copy-start(f32[512]{0:T(512)S(1)} %fusion.93) | copy-start | bytes 6148
  99.1 73.0 %copy-start.62 = (f32[48]{0:T(128)}, f32[48]{0:T(128)S(1)}, u32[]{:S(2)}) copy-start(f32[48]{0:T(128)S(1)} %exponential_negate_fusion) | copy-start | bytes 580
  99.1 63.7 %copy-start.56 = (f32[512]{0:T(512)}, f32[512]{0:T(512)S(1)}, u32[]{:S(2)}) copy-start(f32[512]{0:T(512)S(1)} %fusion.159) | copy-start | bytes 6148
  169.9 3.9 collective-permute-start
  265.3 22.7 %copy-start.66 = (f32[48]{0:T(128)}, f32[48]{0:T(128)S(1)}, u32[]{:S(2)}) copy-start(f32[48]{0:T(128)S(1)} %get-tuple-element.742) | copy-start | bytes 580
  267.4 130.5 %all-gather.13.cloned.1.call-start = ((), (), s32[]{:S(2)}) async-start(), calls=%async_computation.4 | async-start | bytes 9732096 | tf_op jit(solution)/shard_map/all_gather | solution.py:189
  268.1 226.2 %all-gather.15.cloned.1.call-start = ((), (), s32[]{:S(2)}) async-start(), calls=%async_computation.7 | async-start | bytes 3932160 | tf_op jit(solution)/shard_map/all_gather | solution.py:47
  268.9 140.4 %copy-start.47 = (f32[3072]{0:T(1024)}, f32[3072]{0:T(1024)S(1)}, u32[]{:S(2)}) copy-start(f32[3072]{0:T(1024)S(1)} %convert_element_type.99) | copy-start | bytes 36868
  271.4 26.0 %copy-start.20 = (f32[2,256,128,1]{2,1,3,0:T(8,128)}, f32[2,256,128,1]{2,1,3,0:T(8,128)S(1)}, u32[]{:S(2)}) copy-start(f32[2,256,128,1]{2,1,3,0:T(8,128)S(1)} %copy.299) | copy-start | bytes 786436
  320.8 180.3 %copy-start.2 = (f32[1,48,64,128]{3,2,1,0:T(8,128)}, f32[1,48,64,128]{3,2,1,0:T(8,128)S(1)}, u32[]{:S(2)}) copy-start(f32[1,48,64,128]{3,2,1,0:T(8,128)S(1)} %get-tuple-element.515) | copy-start | bytes 4718596
  341.1 56.8 %copy-start.29 = (bf16[1,512,1536]{2,1,0:T(8,128)(2,1)S(1)}, bf16[1,512,1536]{2,1,0:T(8,128)(2,1)}, u32[]{:S(2)}) copy-start(bf16[1,512,1536]{2,1,0:T(8,128)(2,1)} %param.31) | copy-start | bytes 4718596
  348.9 60.4 %copy-start.54 = (f32[512]{0:T(512)}, f32[512]{0:T(512)S(1)}, u32[]{:S(2)}) copy-start(f32[512]{0:T(512)S(1)} %fusion.160) | copy-start | bytes 6148
  430.6 628.9 %all-reduce.33.cloned.1.call-start = ((), (), s32[]{:S(2)}) async-start(), calls=%async_computation.8 | async-start | bytes 183296
  451.8 33.3 %copy-start.14 = (f32[1,1,48,64,128]{4,3,2,1,0:T(8,128)}, f32[1,1,48,64,128]{4,3,2,1,0:T(8,128)S(1)}, u32[]{:S(2)}) copy-start(f32[1,1,48,64,128]{4,3,2,1,0:T(8,128)S(1)} %slice_add_fusion.3) | copy-start | bytes 4718596
  556.0 19.5 %copy-start.32 = (f32[2,256,128]{2,1,0:T(8,128)S(1)}, f32[2,256,128]{2,1,0:T(8,128)}, u32[]{:S(2)}) copy-start(f32[2,256,128]{2,1,0:T(8,128)} %get-tuple-element.1269) | copy-start | bytes 786436 | tf_op jit(solution)/shard_map/transpose(jvp())/while
  556.0 19.9 %copy-start = (f32[48,64,128]{2,1,0:T(8,128)S(1)}, f32[48,64,128]{2,1,0:T(8,128)}, u32[]{:S(2)}) copy-start(f32[48,64,128]{2,1,0:T(8,128)} %dynamic-slice_bitcast_fusion.22) | copy-start | bytes 4718596 | tf_op jit(solution)/shard_map/transpose(jvp())/while
  687.7 19.5 %copy-start.32 = (f32[2,256,128]{2,1,0:T(8,128)S(1)}, f32[2,256,128]{2,1,0:T(8,128)}, u32[]{:S(2)}) copy-start(f32[2,256,128]{2,1,0:T(8,128)} %get-tuple-element.1269) | copy-start | bytes 786436 | tf_op jit(solution)/shard_map/transpose(jvp())/while
  687.7 19.9 %copy-start = (f32[48,64,128]{2,1,0:T(8,128)S(1)}, f32[48,64,128]{2,1,0:T(8,128)}, u32[]{:S(2)}) copy-start(f32[48,64,128]{2,1,0:T(8,128)} %dynamic-slice_bitcast_fusion.22) | copy-start | bytes 4718596 | tf_op jit(solution)/shard_map/transpose(jvp())/while
  847.4 25.2 %copy-start.40 = (f32[3328]{0:T(1024)S(1)}, f32[3328]{0:T(1024)}, u32[]{:S(2)}) copy-start(f32[3328]{0:T(1024)} %copy-done.39) | copy-start | bytes 39940
  847.4 25.2 %copy-start.42 = (f32[3328]{0:T(1024)S(1)}, f32[3328]{0:T(1024)}, u32[]{:S(2)}) copy-start(f32[3328]{0:T(1024)} %copy-done.41) | copy-start | bytes 39940
  847.4 25.2 %copy-start.44 = (f32[3328]{0:T(1024)S(1)}, f32[3328]{0:T(1024)}, u32[]{:S(2)}) copy-start(f32[3328]{0:T(1024)} %copy-done.43) | copy-start | bytes 39940
  847.4 25.2 %copy-start.46 = (f32[3328]{0:T(1024)S(1)}, f32[3328]{0:T(1024)}, u32[]{:S(2)}) copy-start(f32[3328]{0:T(1024)} %copy-done.45) | copy-start | bytes 39940
  898.3 11.1 collective-permute-start.1
  934.4 339.7 %reduce-scatter.6.cloned.1.call-start = ((), (), s32[]{:S(2)}) async-start(), calls=%async_computation.6 | async-start | bytes 19464192 | tf_op jit(solution)/shard_map/reduce_scatter | solution.py:293
  946.7 697.2 %reduce-scatter.4.cloned.1.call-start = ((), (), s32[]{:S(2)}) async-start(), calls=%async_computation.5 | async-start | bytes 41361408 | tf_op jit(solution)/shard_map/reduce_scatter | solution.py:292
  (62 other events, 485.3 us)
Sparse Core Ops, SparseCore 0:
  10.9 133.6 all-gather.8
  267.5 46.0 all-gather.10
  316.5 81.3 all-gather.12
  430.7 27.0 all-gather.14
  934.5 124.9 all-reduce.32
  1066.4 207.7 reduce-scatter.5
  1281.2 362.6 reduce-scatter.3
where the time goes:
time: 1670 us; the launch traced here: 1650 us
  waiting for transfers between devices  765 us (46%)
  matrix products  295 us (18%)
  local copies, waits for them, and re-layouts  261 us (16%)
  other arithmetic  184 us (11%)
  blocking collectives  100 us (6%)
  loops' own time  29.4 us (2%)
    reduce_scatter x1, waiting for transfers between devices, per_device(): lax.psum_scatter(grad_in_w, ('batch', 'seq'), scatter_dimension=0, tiled=...  370 us
    reduce_scatter x1, waiting for transfers between devices, per_device(): lax.psum_scatter(grad_out_w, ('batch', 'seq'), scatter_dimension=0, tiled...  209 us
    dynamic_update_slice x8, local copies, waits for them, and re-layouts, local_states(): lax.map(jax.checkpoint(block_terms), (scaled_x, write_blocks, read_blocks...  138 us
    dot_general x6, matrix products, block_terms(): jnp.einsum('hts,shp->thp', weights * scores[None], x_part, precision=HIGH...  92.6 us
    unnamed x8, waiting for transfers between devices  78.5 us
    unnamed x3, blocking collectives  58.1 us
    all_gather x1, waiting for transfers between devices, per_device(): lax.all_gather(out_proj, ('batch', 'seq'), axis=0, tiled=True)  49 us
    all_gather x1, waiting for transfers between devices, per_device(): lax.all_gather(in_proj, ('batch', 'seq'), axis=0, tiled=True)  45.5 us
  transfers between devices with their start and end apart: 9, of which 6 were waited for; matrix products, arithmetic and copies ran while one was open for 11% of the time, Pallas kernels for 0%

commit v1 on v0

v1 whole, which is shorter than its diff:
```python
import functools

import jax
import jax.numpy as jnp
from jax import lax
from jax.experimental import pallas as pl
from jax.experimental.pallas import tpu as pltpu
from jax.sharding import PartitionSpec as P

EPSILON = 1e-05
HIGHEST = lax.Precision.HIGHEST
AXES = ("batch", "seq")
F32 = jnp.float32
BF16 = jnp.bfloat16
L = 128
LANES = 128

PG, PS, PM, PO, PC = 3, 3, 3, 1, 1
ENTER = F32 if PS > 1 else BF16
VMEM_LIMIT = 60 * 1024 * 1024


def dot(a, b, ca=1, cb=0):
    return lax.dot_general(a, b, (((ca,), (cb,)), ((), ())), preferred_element_type=F32)


def halves(a):
    high = a.astype(BF16)
    return high, (a - high.astype(F32)).astype(BF16)


def mm(a, b, ca=1, cb=0, parts=1):
    if parts == 1:
        return dot(a.astype(BF16), b.astype(BF16), ca, cb)
    a_high, a_low = halves(a)
    b_high, b_low = halves(b)
    return dot(a_high, b_high, ca, cb) + (dot(a_low, b_high, ca, cb) + dot(a_high, b_low, ca, cb))


def dot_exact(a, b):
    return lax.dot_general(
        a, b, (((1,), (0,)), ((), ())), precision=HIGHEST, preferred_element_type=F32
    )


def dot_split(a, b):
    high = a.astype(BF16)
    low = (a - high.astype(F32)).astype(BF16)
    return dot(high, b) + dot(low, b)


def rounded(a, parts):
    return a if parts > 1 else a.astype(BF16).astype(F32)


def iota(shape, dim):
    return lax.broadcasted_iota(jnp.int32, shape, dim)


def sigmoid(v):
    return 1.0 / (1.0 + jnp.exp(-v))


def softplus(v):
    return jnp.maximum(v, 0.0) + jnp.log1p(jnp.exp(-jnp.abs(v)))


def column(value, lane):
    return jnp.broadcast_to(value[:, lane : lane + 1], (value.shape[0], LANES))


def pair_lanes(first, second):
    return jnp.where(iota(first.shape, 1) < LANES // 2, first, second)


def earlier(value, tail, steps):
    turned = pltpu.roll(value, steps, 0)
    head = jnp.where(iota(tail.shape, 0) < steps, pltpu.roll(tail, steps, 0), turned[:8])
    return jnp.concatenate([head, turned[8:]], axis=0)


def later(value, following, steps):
    rows = value.shape[0]
    turned = pltpu.roll(value, rows - steps, 0)
    end = jnp.where(
        iota(following.shape, 0) >= 8 - steps,
        pltpu.roll(following, 8 - steps, 0),
        turned[rows - 8 :],
    )
    return jnp.concatenate([turned[: rows - 8], end], axis=0)


def forward_body(
    width, state, taps, per_seq, p_ref, conv_ref, head_ref, lane_ref,
    v_ref, y_ref, u_ref, square_ref, enter_ref, tail, run,
):
    channels = width + 2 * state
    pairs = width // LANES

    @pl.when(pl.program_id(0) % per_seq == 0)
    def _():
        tail[...] = jnp.zeros_like(tail)
        run[...] = jnp.zeros_like(run)

    conv_in = p_ref[:, width : width + channels]
    before = tail[...]
    convolved = conv_ref[taps : taps + 1] + conv_ref[taps - 1 : taps] * conv_in
    for steps in range(1, taps):
        convolved = convolved + conv_ref[taps - 1 - steps : taps - steps] * earlier(
            conv_in, before, steps
        )
    tail[...] = conv_in[L - 8 :]
    v_ref[...] = convolved
    active = convolved * sigmoid(convolved)
    x = active[:, :width]
    write = active[:, width : width + state]
    read = active[:, width + state :]
    step = softplus(p_ref[:, width + channels :] + head_ref[0:1])
    causal = iota((L, L), 0) >= iota((L, L), 1)
    cum = dot_exact(causal.astype(F32), step * head_ref[1:2])
    cum_rows = cum.T
    scores = mm(read, write, 1, 1, PG)
    running = run[...]
    enter_ref[...] = running.astype(enter_ref.dtype)
    carried = mm(read, running, 1, 0, PS)
    first_half = iota((L, LANES), 1) < LANES // 2
    to_state, decays, y_parts = [], [], []
    for q in range(pairs):
        weights, columns = [], []
        for h in (2 * q, 2 * q + 1):
            col = column(cum, h)
            columns.append(col)
            gap = jnp.where(causal, col - cum_rows[h : h + 1], -jnp.inf)
            weights.append(jnp.exp(gap) * scores)
        cum_pair = pair_lanes(*columns)
        step_pair = pair_lanes(column(step, 2 * q), column(step, 2 * q + 1))
        span = slice(q * LANES, (q + 1) * LANES)
        scaled = x[:, span] * step_pair
        inside = mm(
            jnp.concatenate(weights, axis=1),
            jnp.concatenate(
                [jnp.where(first_half, scaled, 0.0), jnp.where(first_half, 0.0, scaled)], axis=0
            ),
            1, 0, PM,
        )
        last = cum_pair[L - 1 :]
        to_state.append(scaled * jnp.exp(last - cum_pair))
        decays.append(jnp.exp(last))
        y_parts.append(inside + jnp.exp(cum_pair) * carried[:, span])
    y = jnp.concatenate(y_parts, axis=1)
    y_ref[...] = y
    run[...] = jnp.concatenate(decays, axis=1) * running + mm(
        write, jnp.concatenate(to_state, axis=1), 0, 0, PS
    )
    gate = p_ref[:, :width]
    mixed = y + lane_ref[0:1] * x
    gated = mixed * (gate * sigmoid(gate))
    u_ref[...] = (gated * lane_ref[1:2]).astype(BF16)
    squares = gated * gated
    total = squares[:, :LANES]
    for q in range(1, pairs):
        total = total + squares[:, q * LANES : (q + 1) * LANES]
    square_ref[...] = total


def backward_body(
    width, state, taps, per_seq, p_ref, v_ref, y_ref, enter_ref, grad_ref, stat_ref,
    conv_ref, head_ref, lane_ref, expand_ref,
    gp_ref, conv_acc, lane_acc, head_acc, ahead, run, leaving,
):
    channels = width + 2 * state
    pairs = width // LANES

    @pl.when(pl.program_id(0) == 0)
    def _():
        conv_acc[...] = jnp.zeros_like(conv_acc)
        lane_acc[...] = jnp.zeros_like(lane_acc)
        head_acc[...] = jnp.zeros_like(head_acc)

    @pl.when(pl.program_id(0) % per_seq == 0)
    def _():
        ahead[...] = jnp.zeros_like(ahead)
        run[...] = jnp.zeros_like(run)
        leaving[...] = jnp.zeros_like(leaving)

    convolved = v_ref[...]
    bend = sigmoid(convolved)
    active = convolved * bend
    slope = bend * (1.0 + convolved * (1.0 - bend))
    x = active[:, :width]
    write = active[:, width : width + state]
    read = active[:, width + state :]
    raw = p_ref[:, width + channels :] + head_ref[0:1]
    rate = head_ref[1:2]
    step = softplus(raw)
    log_decay = step * rate
    upper = iota((L, L), 0) <= iota((L, L), 1)
    lower = iota((L, L), 0) >= iota((L, L), 1)
    cum = dot_exact(lower.astype(F32), log_decay)
    cum_rows = cum.T

    gate = p_ref[:, :width]
    y = y_ref[...]
    grad = grad_ref[...]
    gate_bend = sigmoid(gate)
    gate_silu = gate * gate_bend
    mixed = y + lane_ref[0:1] * x
    gated = mixed * gate_silu
    inverse = jnp.broadcast_to(stat_ref[:, 0:1], (L, width))
    pull = jnp.broadcast_to(stat_ref[:, 1:2], (L, width))
    scaled_grad = inverse * grad
    grad_gated = scaled_grad * lane_ref[1:2] - gated * pull
    gp_ref[:, :width] = (
        grad_gated * mixed * (gate_bend * (1.0 + gate * (1.0 - gate_bend)))
    ).astype(BF16)
    grad_y = grad_gated * gate_silu
    lane_acc[0:1] += jnp.sum(scaled_grad * gated, axis=0, keepdims=True)
    lane_acc[1:2] += jnp.sum(grad_y * x, axis=0, keepdims=True)
    grad_low = rounded(grad_y, PM)

    scores = mm(write, read, 1, 1, PG)
    grad_state = run[...]
    from_state = mm(write, grad_state, 1, 0, PS)
    entering = enter_ref[...]
    first_half = iota((L, LANES), 1) < LANES // 2
    grad_scores = jnp.zeros((L, L), F32)
    to_state, grad_carried, decays, grad_scaled, lows, steps = [], [], [], [], [], []
    for q in range(pairs):
        span = slice(q * LANES, (q + 1) * LANES)
        step_pair = pair_lanes(column(step, 2 * q), column(step, 2 * q + 1))
        scaled = x[:, span] * step_pair
        low = rounded(scaled, PM)
        dy = grad_low[:, span]
        outer = mm(
            jnp.concatenate(
                [jnp.where(first_half, low, 0.0), jnp.where(first_half, 0.0, low)], axis=0
            ),
            dy,
            1,
            1,
            PO,
        )
        weights, columns = [], []
        for k in range(2):
            h = 2 * q + k
            col = column(cum, h)
            columns.append(col)
            decay = jnp.exp(jnp.where(upper, cum_rows[h : h + 1] - col, -jnp.inf))
            weights.append(decay * scores)
            grad_scores = grad_scores + decay * outer[k * L : (k + 1) * L]
        inside = mm(
            jnp.concatenate(weights, axis=1),
            jnp.concatenate(
                [jnp.where(first_half, dy, 0.0), jnp.where(first_half, 0.0, dy)], axis=0
            ),
            1,
            0,
            PM,
        )
        cum_pair = pair_lanes(*columns)
        last = cum_pair[L - 1 :]
        to_end = jnp.exp(last - cum_pair)
        to_state.append(scaled * to_end)
        grad_carried.append(grad_y[:, span] * jnp.exp(cum_pair))
        decays.append(jnp.exp(last))
        grad_scaled.append(inside + to_end * from_state[:, span])
        lows.append(low)
        steps.append(step_pair)
    grad_scaled = jnp.concatenate(grad_scaled, axis=1)
    to_state = jnp.concatenate(to_state, axis=1)
    grad_carried = jnp.concatenate(grad_carried, axis=1)
    lows = jnp.concatenate(lows, axis=1)
    steps = jnp.concatenate(steps, axis=1)
    grad_write = mm(grad_scores, read, 1, 0, PO) + mm(to_state, grad_state, 1, 1, PC)
    grad_read = mm(grad_scores, write, 0, 0, PO) + mm(grad_carried, entering, 1, 1, PC)
    across = jnp.sum(leaving[...].astype(F32) * grad_state, axis=0, keepdims=True)
    run[...] = jnp.concatenate(decays, axis=1) * grad_state + mm(read, grad_carried, 0, 0, PS)
    leaving[...] = entering

    rows = jnp.concatenate(
        [
            y * grad_low - lows * grad_scaled,
            x * grad_scaled,
            jnp.broadcast_to(across, (8, width)),
        ],
        axis=0,
    )
    by_head = dot_split(rows, expand_ref[...])
    grad_decay = dot_split_left(upper.astype(BF16), by_head[:L]) + by_head[2 * L : 2 * L + 1]
    grad_step = by_head[L : 2 * L] + rate * grad_decay
    grad_raw = grad_step * sigmoid(raw)
    head_acc[0:1] += jnp.sum(grad_raw, axis=0, keepdims=True)
    head_acc[1:2] += jnp.sum(grad_decay * log_decay, axis=0, keepdims=True)
    gp_ref[:, width + channels :] = grad_raw.astype(BF16)

    grad_x = grad_scaled * steps + lane_ref[0:1] * grad_y
    grad_conv = jnp.concatenate([grad_x, grad_write, grad_read], axis=1) * slope
    following = ahead[...]
    conv_in = p_ref[:, width : width + channels]
    total = conv_ref[taps - 1 : taps] * grad_conv
    conv_acc[taps - 1 : taps] += jnp.sum(grad_conv * conv_in, axis=0, keepdims=True)
    conv_acc[taps : taps + 1] += jnp.sum(grad_conv, axis=0, keepdims=True)
    for steps_on in range(1, taps):
        moved = later(grad_conv, following, steps_on)
        row = taps - 1 - steps_on
        total = total + conv_ref[row : row + 1] * moved
        conv_acc[row : row + 1] += jnp.sum(moved * conv_in, axis=0, keepdims=True)
    ahead[...] = grad_conv[:8]
    gp_ref[:, width : width + channels] = total.astype(BF16)


def dot_split_left(a, b):
    high = b.astype(BF16)
    low = (b - high.astype(F32)).astype(BF16)
    return dot(a, high) + dot(a, low)


def forward_scan(projected, conv_rows, head_rows, lane_rows, width, state, taps, per_seq):
    tokens, columns = projected.shape
    blocks = tokens // L
    channels = width + 2 * state
    whole = lambda i: (0, 0)
    mine = lambda i: (i, 0)
    return pl.pallas_call(
        functools.partial(forward_body, width, state, taps, per_seq),
        grid=(blocks,),
        in_specs=[
            pl.BlockSpec((L, columns), mine),
            pl.BlockSpec(conv_rows.shape, whole),
            pl.BlockSpec(head_rows.shape, whole),
            pl.BlockSpec(lane_rows.shape, whole),
        ],
        out_specs=[
            pl.BlockSpec((L, channels), mine),
            pl.BlockSpec((L, width), mine),
            pl.BlockSpec((L, width), mine),
            pl.BlockSpec((L, LANES), mine),
            pl.BlockSpec((state, width), mine),
        ],
        out_shape=[
            jax.ShapeDtypeStruct((tokens, channels), F32),
            jax.ShapeDtypeStruct((tokens, width), F32),
            jax.ShapeDtypeStruct((tokens, width), BF16),
            jax.ShapeDtypeStruct((tokens, LANES), F32),
            jax.ShapeDtypeStruct((blocks * state, width), ENTER),
        ],
        scratch_shapes=[pltpu.VMEM((8, channels), F32), pltpu.VMEM((state, width), F32)],
        compiler_params=pltpu.CompilerParams(
            dimension_semantics=("arbitrary",), vmem_limit_bytes=VMEM_LIMIT
        ),
        cost_estimate=pl.CostEstimate(
            flops=tokens * width * 1024, bytes_accessed=tokens * columns * 10, transcendentals=0
        ),
        name="forward_scan",
    )(projected, conv_rows, head_rows, lane_rows)


def backward_scan(
    projected, convolved, y, entering, grad, stats, conv_rows, head_rows, lane_rows, expand,
    width, state, taps, per_seq,
):
    tokens, columns = projected.shape
    blocks = tokens // L
    channels = width + 2 * state
    whole = lambda i: (0, 0)
    mine = lambda i: (blocks - 1 - i, 0)
    return pl.pallas_call(
        functools.partial(backward_body, width, state, taps, per_seq),
        grid=(blocks,),
        in_specs=[
            pl.BlockSpec((L, columns), mine),
            pl.BlockSpec((L, channels), mine),
            pl.BlockSpec((L, width), mine),
            pl.BlockSpec((state, width), mine),
            pl.BlockSpec((L, width), mine),
            pl.BlockSpec((L, stats.shape[1]), mine),
            pl.BlockSpec(conv_rows.shape, whole),
            pl.BlockSpec(head_rows.shape, whole),
            pl.BlockSpec(lane_rows.shape, whole),
            pl.BlockSpec(expand.shape, whole),
        ],
        out_specs=[
            pl.BlockSpec((L, columns), mine),
            pl.BlockSpec(conv_rows.shape, whole),
            pl.BlockSpec(lane_rows.shape, whole),
            pl.BlockSpec(head_rows.shape, whole),
        ],
        out_shape=[
            jax.ShapeDtypeStruct((tokens, columns), BF16),
            jax.ShapeDtypeStruct(conv_rows.shape, F32),
            jax.ShapeDtypeStruct(lane_rows.shape, F32),
            jax.ShapeDtypeStruct(head_rows.shape, F32),
        ],
        scratch_shapes=[
            pltpu.VMEM((8, channels), F32),
            pltpu.VMEM((state, width), F32),
            pltpu.VMEM((state, width), ENTER),
        ],
        compiler_params=pltpu.CompilerParams(
            dimension_semantics=("arbitrary",), vmem_limit_bytes=VMEM_LIMIT
        ),
        cost_estimate=pl.CostEstimate(
            flops=tokens * width * 3072, bytes_accessed=tokens * columns * 14, transcendentals=0
        ),
        name="backward_scan",
    )(projected, convolved, y, entering, grad, stats, conv_rows, head_rows, lane_rows, expand)


def rows_of(vectors, lanes):
    made = [jnp.pad(v.astype(F32), ((0, 0), (0, lanes - v.shape[1]))) for v in vectors]
    stacked = jnp.concatenate(made, axis=0)
    return jnp.pad(stacked, ((0, 8 - stacked.shape[0]), (0, 0)))


def send(value, sizes, move):
    nb, ns = sizes
    pairs = []
    for b in range(nb):
        for s in range(ns):
            goal = move(b, s)
            if goal is not None:
                pairs.append((b * ns + s, goal[0] * ns + goal[1]))
    return lax.ppermute(value, AXES, pairs)


def swap_core(value, sizes):
    return send(value, sizes, lambda b, s: (b, s ^ 1))


def turn_row(value, sizes, k):
    return send(value, sizes, lambda b, s: (b, (s + 2 * k) % sizes[1]))


def gather_pieces(piece, sizes):
    ns = sizes[1]
    me = lax.axis_index("seq")
    place = lambda total, part, at: lax.dynamic_update_index_in_dim(total, part, at, 0)
    total = jnp.zeros((ns,) + piece.shape, piece.dtype)
    got = [piece] + [turn_row(piece, sizes, k) for k in range(1, ns // 2)]
    for k, part in enumerate(got):
        at = (me + ns - 2 * k) % ns
        total = place(total, part, at)
        total = place(total, swap_core(part, sizes), at ^ 1)
    return total


def scatter_pieces(value, sizes):
    ns = sizes[1]
    me = lax.axis_index("seq")
    chip, core = me // 2, me % 2
    split = value.reshape((ns // 2, 2) + value.shape[1:])
    give = lax.dynamic_index_in_dim(split, 1 - core, 1, False).astype(BF16)
    keep = lax.dynamic_index_in_dim(split, core, 1, False)
    both = keep + swap_core(give, sizes).astype(F32)
    total = lax.dynamic_index_in_dim(both, chip, 0, False)
    for k in range(1, ns // 2):
        part = lax.dynamic_index_in_dim(both, (chip + k) % (ns // 2), 0, False)
        total = total + turn_row(part.astype(BF16), sizes, k).astype(F32)
    return total


def add_over(value, sizes, axis):
    k = 1
    while k < sizes[axis]:
        step = k
        if axis == 0:
            value = value + send(value, sizes, lambda b, s: (b ^ step, s))
        else:
            value = value + send(value, sizes, lambda b, s: (b, s ^ step))
        k *= 2
    return value


def collect_over_seq(value, sizes):
    ns = sizes[1]
    me = lax.axis_index("seq")
    total = lax.dynamic_update_index_in_dim(
        jnp.zeros((ns,) + value.shape, value.dtype), value, me, 0
    )
    return add_over(total, sizes, 1)


def per_device(
    sizes, hidden, in_proj, out_proj, conv_weight, conv_bias, step_bias, decay_log,
    skip_weight, gated_gain, norm_gain, cotangent,
):
    nb, ns = sizes
    devices = nb * ns
    me_b, me_s = lax.axis_index("batch"), lax.axis_index("seq")
    seq_count, piece, model = hidden.shape
    taps, conv_part = conv_weight.shape
    conv_channels = conv_part * devices
    inner = out_proj.shape[0] * devices
    heads = step_bias.shape[0]
    state = (conv_channels - inner) // 2
    in_rows = in_proj.shape[0]
    own_heads = heads // ns
    width = inner // ns
    head_size = inner // heads
    channels = width + 2 * state
    columns = width + channels + LANES
    tokens = seq_count * piece * ns
    per_seq = piece * ns // L

    dt_at = inner + conv_channels
    payload = jnp.stack(
        [
            jnp.concatenate(
                [
                    in_proj[:, s * width : (s + 1) * width],
                    in_proj[:, inner + s * width : inner + (s + 1) * width],
                    in_proj[:, 2 * inner : dt_at],
                    jnp.pad(
                        in_proj[:, dt_at + s * own_heads : dt_at + (s + 1) * own_heads],
                        ((0, 0), (0, LANES - own_heads)),
                    ),
                ],
                axis=1,
            )
            for s in range(ns)
        ]
    )
    mine = lax.all_to_all(payload, "seq", 0, 0, tiled=False).reshape(ns * in_rows, columns)
    weight_in = lax.all_gather(mine, "batch", axis=0, tiled=True)
    out_rows = lax.ppermute(
        out_proj, AXES, [(j, (j % nb) * ns + j // nb) for j in range(devices)]
    )
    weight_out = lax.all_gather(out_rows, "batch", axis=0, tiled=True)

    small = jnp.concatenate(
        [conv_weight.reshape(-1), conv_bias.reshape(-1), gated_gain, norm_gain]
    ).reshape(1, -1)
    small = lax.all_gather(small, "seq", axis=0, tiled=True)
    small = lax.all_gather(small, "batch", axis=0, tiled=True).astype(F32)
    conv_all = jnp.moveaxis(
        small[:, : taps * conv_part].reshape(devices, taps, conv_part), 0, 1
    ).reshape(taps, conv_channels)
    at = taps * conv_part
    bias_all = small[:, at : at + conv_part].reshape(1, conv_channels)
    at += conv_part
    gain_all = small[:, at : at + gated_gain.shape[0]].reshape(1, inner)
    at += gated_gain.shape[0]
    norm_all = small[:, at:].reshape(1, model)
    conv_all = jnp.concatenate([conv_all, bias_all], axis=0)
    conv_rows = rows_of(
        [
            jnp.concatenate(
                [
                    lax.dynamic_slice_in_dim(conv_all, me_s * width, width, 1),
                    conv_all[:, inner:],
                ],
                axis=1,
            )
        ],
        channels,
    )
    own = lambda v: lax.dynamic_slice_in_dim(v, me_s * own_heads, own_heads, 0)
    head_rows = rows_of([own(step_bias)[None], -jnp.exp(own(decay_log))[None]], LANES)
    lane_rows = rows_of(
        [
            jnp.repeat(own(skip_weight), head_size)[None],
            lax.dynamic_slice_in_dim(gain_all, me_s * width, width, 1),
        ],
        width,
    )
    expand = (
        jnp.arange(width)[:, None] // head_size == jnp.arange(LANES)[None, :]
    ).astype(BF16)

    stream = hidden.reshape(-1, model).astype(F32)
    spread = lax.rsqrt(jnp.mean(stream * stream, axis=-1, keepdims=True) + EPSILON)
    normed = (stream * spread * norm_all).astype(BF16)

    def in_order(pieces):
        value = pieces.reshape((ns, seq_count, piece, model))
        return jnp.swapaxes(value, 0, 1).reshape(tokens, model)

    def in_pieces(value):
        value = value.reshape((seq_count, ns, piece, model))
        return jnp.swapaxes(value, 0, 1).reshape(ns, seq_count * piece, model)

    normed_all = in_order(gather_pieces(normed, sizes))
    upstream = in_order(gather_pieces(cotangent.reshape(-1, model), sizes))

    projected = jnp.dot(normed_all, weight_in, preferred_element_type=F32)
    convolved, y, ungained, squares, entering = forward_scan(
        projected, conv_rows, head_rows, lane_rows, width, state, taps, per_seq
    )
    grad_gated = jnp.einsum("td,kd->tk", upstream, weight_out, preferred_element_type=F32)
    sums = jnp.stack(
        [
            jnp.sum(squares, axis=1),
            jnp.sum(grad_gated * ungained.astype(F32), axis=1),
        ]
    )
    sums = add_over(sums, sizes, 1)
    inverse = lax.rsqrt(sums[0] / inner + EPSILON)
    pull = inverse * inverse * inverse * sums[1] / inner
    stats = jnp.stack([inverse, pull], axis=1)
    out_partial = jnp.dot(ungained, weight_out, preferred_element_type=F32)
    out_sum = scatter_pieces(in_pieces(out_partial), sizes)
    own_inverse = lax.dynamic_index_in_dim(
        jnp.swapaxes(inverse.reshape(seq_count, ns, piece), 0, 1), me_s, 0, False
    ).reshape(-1, 1)
    result = (stream + own_inverse * out_sum).astype(BF16)
    gated_low = (ungained.astype(F32) * inverse[:, None]).astype(BF16)
    grad_out_w = jnp.einsum("tk,td->kd", gated_low, upstream, preferred_element_type=F32)

    grad_proj, conv_acc, lane_acc, head_acc = backward_scan(
        projected, convolved, y, entering, grad_gated, stats, conv_rows, head_rows, lane_rows,
        expand, width, state, taps, per_seq,
    )
    grad_in_w = jnp.einsum("td,tk->dk", normed_all, grad_proj, preferred_element_type=F32)
    grad_normed = jnp.einsum("tk,dk->td", grad_proj, weight_in, preferred_element_type=F32)
    grad_normed = scatter_pieces(in_pieces(grad_normed), sizes)
    scaled = grad_normed * norm_all
    unit = stream * spread
    grad_stream = spread * (scaled - unit * jnp.mean(scaled * unit, axis=-1, keepdims=True))
    hidden_grad = (cotangent.reshape(-1, model).astype(F32) + grad_stream).astype(BF16)

    out_part = lax.psum_scatter(
        grad_out_w.astype(BF16), "batch", scatter_dimension=0, tiled=True
    )
    out_proj_grad = lax.ppermute(
        out_part, AXES, [((j % nb) * ns + j // nb, j) for j in range(devices)]
    ).astype(F32)
    in_part = lax.psum_scatter(grad_in_w.astype(BF16), "batch", scatter_dimension=0, tiled=True)
    by_source = lax.all_to_all(
        in_part.reshape(ns, in_rows, columns), "seq", 0, 0, tiled=False
    ).astype(F32)
    across = lambda lo, hi: jnp.concatenate([by_source[s, :, lo:hi] for s in range(ns)], axis=1)
    in_proj_grad = jnp.concatenate(
        [
            across(0, width),
            across(width, 2 * width),
            jnp.sum(by_source[:, :, 2 * width : width + channels], axis=0),
            across(width + channels, width + channels + own_heads),
        ],
        axis=1,
    )
    norm_gain_grad = jnp.sum(in_proj.astype(F32) * in_proj_grad, axis=1) / norm_gain.astype(F32)

    by_head = jnp.sum(lane_acc[1].reshape(own_heads, head_size), axis=1)
    packed = jnp.concatenate(
        [
            conv_acc[: taps + 1].reshape(-1),
            lane_acc[0],
            by_head,
            head_acc[0, :own_heads],
            head_acc[1, :own_heads],
        ]
    )
    packed = jnp.pad(packed, (0, -packed.shape[0] % (8 * LANES))).reshape(-1, LANES)
    packed = collect_over_seq(add_over(packed, sizes, 0), sizes).reshape(ns, -1)
    rows = (taps + 1) * channels
    conv_grads = packed[:, :rows].reshape(ns, taps + 1, channels)
    conv_grads = jnp.concatenate(
        [
            jnp.moveaxis(conv_grads[:, :, :width], 0, 1).reshape(taps + 1, inner),
            jnp.sum(conv_grads[:, :, width:], axis=0),
        ],
        axis=1,
    )
    me = me_b * ns + me_s
    conv_grads = lax.dynamic_slice_in_dim(conv_grads, me * conv_part, conv_part, 1)
    gain_grad = lax.dynamic_slice_in_dim(
        packed[:, rows : rows + width].reshape(-1), me * gated_gain.shape[0], gated_gain.shape[0], 0
    )
    at = rows + width
    skip_grad, bias_grad, rate_grad = (
        packed[:, at + k * own_heads : at + (k + 1) * own_heads].reshape(-1) for k in range(3)
    )
    return (
        result.reshape(hidden.shape),
        hidden_grad.reshape(hidden.shape),
        in_proj_grad,
        out_proj_grad,
        conv_grads[:taps],
        conv_grads[taps],
        bias_grad,
        rate_grad,
        skip_grad,
        gain_grad,
        norm_gain_grad,
    )


def solution(mesh):
    both = P(AXES)
    in_specs = (
        P("batch", "seq", None),
        P(AXES, None),
        P(AXES, None),
        P(None, AXES),
        both,
        P(),
        P(),
        P(),
        both,
        both,
        P("batch", "seq", None),
    )
    out_specs = (
        P("batch", "seq", None),
        P("batch", "seq", None),
        P(AXES, None),
        P(AXES, None),
        P(None, AXES),
        both,
        P(),
        P(),
        P(),
        both,
        both,
    )
    sizes = (mesh.shape["batch"], mesh.shape["seq"])
    return jax.shard_map(
        functools.partial(per_device, sizes),
        mesh=mesh,
        in_specs=in_specs,
        out_specs=out_specs,
        check_vma=False,
    )
```

time: 1670 us -> 453 us (0.27)
  waiting for transfers between devices: 765 us -> 110 us
  matrix products: 295 us -> 80.9 us
  local copies, waits for them, and re-layouts: 261 us -> 61.6 us
  other arithmetic: 184 us -> 31.8 us
  Pallas kernels: 0 us -> 76.4 us
  blocking collectives: 100 us -> 53.6 us
  loops' own time: 29.4 us -> 0 us
  starting transfers between devices: 4.48 us -> 23 us
    reduce_scatter x2, waiting for transfers between devices: 579 us -> 13.8 us  [the longest x1 13.8 us: per_device(): lax.psum_scatter(grad_in_w.astype(BF16), 'batch', scatter_dimension=0, ti...]
    dot_general x35 -> x6, matrix products: 295 us -> 80.9 us  [the longest x1 19.2 us: per_device(): projected = jnp.dot(normed_all, weight_in, preferred_element_type=F32)]
    dynamic_update_slice x8 -> x7, local copies, waits for them, and re-layouts: 138 us -> 14.6 us  [gather_pieces(): lax.dynamic_update_index_in_dim(total, part, at, 0)]
    all_gather x4 -> x2, waiting for transfers between devices: 107 us -> 0.02 us  [the longest x1 0.02 us: per_device(): weight_out = lax.all_gather(out_rows, 'batch', axis=0, tiled=True)]
    ppermute x2 -> x19, waiting for transfers between devices: 0.01 us -> 94.9 us  [the longest x17 94.9 us: send(): return lax.ppermute(value, AXES, pairs)]
    unnamed x8 -> x4, waiting for transfers between devices: 78.5 us -> 0.07 us
    pallas_call x0 -> x2, Pallas kernels: none -> 76.4 us  [the longest x1 46.5 us: backward_scan(): pl.pallas_call(functools.partial(backward_body, width, state, taps, per_s...]
    reduce_sum x13 -> x7, other arithmetic: 64.6 us -> 5.53 us  [the longest x1 3.22 us: per_device(): jnp.mean(scaled * unit, axis=-1, keepdims=True)]
  transfers between devices with their start and end apart: 9 -> 24, of which waited for: 6 -> 11; matrix products, arithmetic and copies ran while one was open for 11% -> 30% of each run, Pallas kernels for 0% -> 17%
where the time goes in v1:
time: 453 us; the launch traced here: 452 us
  waiting for transfers between devices  110 us (24%)
  matrix products  80.9 us (18%)
  Pallas kernels  76.4 us (17%)
  local copies, waits for them, and re-layouts  61.6 us (14%)
  blocking collectives  53.6 us (12%)
  other arithmetic  31.8 us (7%)
  starting transfers between devices  23 us (5%)
  between operations  15 us (3%)
    ppermute x17, waiting for transfers between devices, send(): return lax.ppermute(value, AXES, pairs)  94.9 us
    pallas_call x1, Pallas kernels, backward_scan(): pl.pallas_call(functools.partial(backward_body, width, state, taps, per_s...  46.5 us
    all_gather x1, blocking collectives, per_device(): small = lax.all_gather(small, 'batch', axis=0, tiled=True).astype(F32)  32.5 us
    pallas_call x1, Pallas kernels, forward_scan(): pl.pallas_call(functools.partial(forward_body, width, state, taps, per_se...  29.9 us
    dot_general x1, matrix products, per_device(): projected = jnp.dot(normed_all, weight_in, preferred_element_type=F32)  19.2 us
    dot_general x1, matrix products, per_device(): jnp.einsum('td,tk->dk', normed_all, grad_proj, preferred_element_type=F32)  18.9 us
    dot_general x1, matrix products, per_device(): jnp.einsum('tk,dk->td', grad_proj, weight_in, preferred_element_type=F32)  17.6 us
    all_to_all x1, blocking collectives, per_device(): lax.all_to_all(payload, 'seq', 0, 0, tiled=False)  15.3 us
  transfers between devices with their start and end apart: 24, of which 11 were waited for; matrix products, arithmetic and copies ran while one was open for 30% of the time, Pallas kernels for 17%

profile of v1, /device:TPU:0, one launch (start us, length us, event | category | flops | bytes accessed | tf_op | source)
XLA Modules:
  0.0 452.0 jit_solution(9521479246687077275)
XLA Ops:
  11.3 15.3 %all_to_all.10 = bf16[4,48,1920]{2,1,0:T(8,128)(2,1)} all-to-all(bf16[4,48,1920]{2,1,0:T(8,128)(2,1)S(1)} %pad_maximum_fusion), channel_id=1, replica_groups=mesh['batch'=8,'seq'=4] {'seq'}, dimensions={0} | all-to-all | bytes 1474560 | tf_op jit(solution)/shard_map/all_to_all | solution.py:523
  28.3 5.8 %all-reduce.10 = bf16[2656]{0:T(1024)(128)(2,1)S(1)} all-reduce(bf16[2656]{0:T(1024)(128)(2,1)S(1)} %dynamic-update-slice.1), channel_id=2, replica_groups=mesh['batch'=8,'seq'=4] {'seq'}, use_global_device_ids=true, to_apply=%add.10 | all-reduce | flops 2656 | bytes 10624
  34.3 32.5 %all-gather.1 = bf16[8,4,664]{2,1,0:T(4,128)(2,1)S(1)} all-gather(bf16[1,4,664]{2,1,0:T(4,128)(2,1)S(1)} %reshape.254), channel_id=1, replica_groups=mesh['batch'=8,'seq'=4] {'batch'}, dimensions={0}, use_global_device_ids=true | all-gather | bytes 47808 | tf_op jit(solution)/shard_map/all_gather | solution.py:534
  81.6 3.1 broadcast.157.clone
  87.6 3.2 broadcast.157.clone.1
  93.1 18.3 %collective-permute-done.1 = bf16[512,1536]{1,0:T(8,128)(2,1)} collective-permute-done((bf16[512,1536]{1,0:T(8,128)(2,1)}, bf16[512,1536]{1,0:T(8,128)(2,1)}, u32[]{:S(2)}, u32[]{:S(2)}) %collective-permute-start.1) | collective-permute-done | bytes 1572896 | tf_op jit(solution)/shard_map/ppermute | solution.py:423
  111.3 25.3 %collective-permute-done.4 = bf16[512,1536]{1,0:T(8,128)(2,1)} collective-permute-done((bf16[512,1536]{1,0:T(8,128)(2,1)S(1)}, bf16[512,1536]{1,0:T(8,128)(2,1)}, u32[]{:S(2)}, u32[]{:S(2)}) %collective-permute-start.4) | collective-permute-done | bytes 1572896 | tf_op jit(solution)/shard_map/ppermute | solution.py:423
  136.7 2.7 bitcast_dynamic-update-slice_fusion.5
  139.4 2.7 bitcast_dynamic-update-slice_fusion.4
  142.1 2.7 bitcast_dynamic-update-slice_fusion.2
  144.8 2.6 bitcast_dynamic-update-slice_fusion.1
  150.0 19.2 %fusion.60.p_ref = f32[2048,1920]{1,0:T(8,128)} fusion(bf16[2048,1536]{1,0:T(8,128)(2,1)} %bitcast.5, bf16[1536,1920]{1,0:T(8,128)(2,1)} %all-gather.5.cloned.1.call-done), kind=kOutput, calls=%fused_computation.138 | convolution fusion | flops 12079595520 | bytes 27918336 | tf_op jit(solution)/shard_map/dot_general | solution.py:585
  169.2 29.9 %forward_scan.1 = (f32[2048,1024]{1,0:T(8,128)}, f32[2048,768]{1,0:T(8,128)}, bf16[2048,768]{1,0:T(8,128)(2,1)}, f32[2048,128]{1,0:T(8,128)}, f32[2048,768]{1,0:T(8,128)}) custom-call(f32[2048,1920]{1,0:T(8,128)} %fusion.60.p_ref, f32[8,1024]{1,0:T(8,128)} %pad.40.conv_ref, f32[8,128]{1,0:T(8,128)} %pad.43.head_ref, f32[8,768]{1,0:T(8,128)} %select_maximum_fusion.1.lane_ref), custom_call_target="tpu_custom_call" | custom-call | flops 1610612736 | bytes 39321600 | tf_op jit(solution)/shard_map/forward_scan/pallas_call | solution.py:324
  200.7 10.7 %fusion = (f32[2048]{0:T(1024)S(1)}, f32[2048,768]{1,0:T(8,128)}) fusion(bf16[2048,768]{1,0:T(8,128)(2,1)} %get-tuple-element.21, bf16[2048,1536]{1,0:T(8,128)(2,1)} %bitcast.19, bf16[768,1536]{1,0:T(8,128)(2,1)} %all-gather.7.cloned.1.call-done), kind=kOutput, calls=%fused_computation.3 | convolution fusion | flops 4836554752 | bytes 18096128 | tf_op jit(solution)/shard_map/td,kd->tk/dot_general | solution.py:589
  217.3 9.3 %convolution_convert_fusion.1 = bf16[768,1536]{1,0:T(8,128)(2,1)} fusion(bf16[2048,1536]{1,0:T(8,128)(2,1)} %bitcast.19, bf16[2048,768]{1,0:T(8,128)(2,1)S(1)} %copy-done.17, f32[2048]{0:T(1024)S(1)} %bitcast.201), kind=kOutput, calls=%fused_computation.17 | convolution fusion | flops 4837736448 | bytes 11804672 | tf_op jit(solution)/shard_map/tk,td->kd/dot_general | solution.py:607
  229.2 46.5 %backward_scan.1 = (bf16[2048,1920]{1,0:T(8,128)(2,1)}, f32[8,1024]{1,0:T(8,128)}, f32[8,768]{1,0:T(8,128)}, f32[8,128]{1,0:T(8,128)}) custom-call(f32[2048,1920]{1,0:T(8,128)} %fusion.60.p_ref, f32[2048,1024]{1,0:T(8,128)} %get-tuple-element.22.v_ref, f32[2048,768]{1,0:T(8,128)} %get-tuple-element.23.y_ref, f32[2048,768]{1,0:T(8,128)} %get-tuple-element.24.enter_ref, ...), custom_call_target="tpu_custom_call" | custom-call | flops 4831838208 | bytes 55050240 | tf_op jit(solution)/shard_map/backward_scan/pallas_call | solution.py:367
  275.7 18.9 %convolution_convert_fusion = bf16[1536,1920]{1,0:T(8,128)(2,1)} fusion(bf16[2048,1536]{1,0:T(8,128)(2,1)} %bitcast.5, bf16[2048,1920]{1,0:T(8,128)(2,1)} %get-tuple-element.25), kind=kOutput, calls=%fused_computation.2 | convolution fusion | flops 12082544640 | bytes 20054016 | tf_op jit(solution)/shard_map/td,tk->dk/dot_general | solution.py:613
  294.6 17.6 %fusion.62 = f32[2048,1536]{1,0:T(8,128)S(1)} fusion(bf16[2048,1920]{1,0:T(8,128)(2,1)} %get-tuple-element.25, bf16[1536,1920]{1,0:T(8,128)(2,1)} %all-gather.5.cloned.1.call-done), kind=kOutput, calls=%fused_computation.140 | convolution fusion | flops 12079595520 | bytes 26345472 | tf_op jit(solution)/shard_map/tk,dk->td/dot_general | solution.py:614
  314.3 5.1 %copy-done.4 = f32[2048,1536]{1,0:T(8,128)} copy-done((f32[2048,1536]{1,0:T(8,128)}, f32[2048,1536]{1,0:T(8,128)S(1)}, u32[]{:S(2)}) %copy-start.4) | copy-done | bytes 12582936
  319.4 5.1 %fusion.61 = f32[2048,1536]{1,0:T(8,128)S(1)} fusion(bf16[2048,768]{1,0:T(8,128)(2,1)S(1)} %copy-done.18, bf16[768,1536]{1,0:T(8,128)(2,1)S(1)} %copy-done.19), kind=kOutput, calls=%fused_computation.139 | convolution fusion | flops 4831838208 | bytes 18087936 | tf_op jit(solution)/shard_map/dot_general | solution.py:600
  324.5 4.5 copy-done.3
  335.3 2.7 collective-permute-done.14
  339.2 3.6 collective-permute-done.15
  345.4 4.0 collective-permute-done.16
  353.2 5.0 %bitcast_add_fusion = f32[2,512,1536]{2,1,0:T(8,128)S(1)} fusion(bf16[2,512,1536]{2,1,0:T(8,128)(2,1)} %collective-permute-done.11, f32[2,2,512,1536]{3,2,1,0:T(8,128)} %bitcast.188, s32[]{:T(128)S(6)} %select_n.111), kind=kLoop, calls=%fused_computation.7 | loop fusion | flops 3145728 | bytes 15728644 | tf_op jit(solution)/shard_map/add | solution.py:454
  359.6 6.2 %bitcast_add_fusion.1 = f32[2,512,1536]{2,1,0:T(8,128)S(1)} fusion(bf16[2,512,1536]{2,1,0:T(8,128)(2,1)} %collective-permute-done.9, f32[2,2,512,1536]{3,2,1,0:T(8,128)} %bitcast.186, s32[]{:T(128)S(6)} %select_n.111), kind=kLoop, calls=%fused_computation.8 | loop fusion | flops 3145728 | bytes 15728644 | tf_op jit(solution)/shard_map/add | solution.py:454
  375.2 25.9 %collective-permute-done.12 = bf16[512,1536]{1,0:T(8,128)(2,1)} collective-permute-done((bf16[512,1536]{1,0:T(8,128)(2,1)}, bf16[512,1536]{1,0:T(8,128)(2,1)}, u32[]{:S(2)}, u32[]{:S(2)}) %collective-permute-start.12) | collective-permute-done | bytes 1572896 | tf_op jit(solution)/shard_map/ppermute | solution.py:423
  401.0 3.2 fusion.9
  404.2 13.8 %reduce-scatter.3.cloned.1.call-done = bf16[192,1920]{1,0:T(8,128)(2,1)} async-done(((bf16[1536,1920]{1,0:T(8,128)(2,1)}), bf16[192,1920]{1,0:T(8,128)(2,1)}) %reduce-scatter.3.cloned.1.call-update) | async-done | bytes 737296 | tf_op jit(solution)/shard_map/reduce_scatter | solution.py:627
  418.0 4.2 all-to-all-start.1
  422.3 12.5 %collective-permute-done.10 = bf16[512,1536]{1,0:T(8,128)(2,1)} collective-permute-done((bf16[512,1536]{1,0:T(8,128)(2,1)}, bf16[512,1536]{1,0:T(8,128)(2,1)}, u32[]{:S(2)}, u32[]{:S(2)}) %collective-permute-start.10) | collective-permute-done | bytes 1572896 | tf_op jit(solution)/shard_map/ppermute | solution.py:423
  434.7 5.7 %fusion.28 = (bf16[1,512,1536]{2,1,0:T(8,128)(2,1)}, bf16[1,512,1536]{2,1,0:T(8,128)(2,1)}) fusion(bf16[1,512,1536]{2,1,0:T(8,128)(2,1)S(1)} %copy-done, bf16[512,1536]{1,0:T(8,128)(2,1)} %collective-permute-done.12, f32[2,512,1536]{2,1,0:T(8,128)} %copy-done.1, s32[]{:T(128)S(6)} %select_n.114, f32[512]{0:T(512)S(1)} %broadcast_multiply_fusion, ...), kind=kLoop, calls=%fused_computation.41 | loop fusion | flops 12582912 | bytes 15740932 | tf_op jit(solution)/shard_map/reshape | solution.py:675
  (178 shorter events, 69.2 us)
Async XLA Ops:
  7.2 142.8 %all-gather.5.cloned.1.call-start = ((), (), s32[]{:S(2)}) async-start(), calls=%async_computation.4 | async-start | bytes 6635520 | tf_op jit(solution)/shard_map/all_gather | solution.py:524
  8.9 17.8 %copy-start.11 = (bf16[4,104]{1,0:T(4,128)(2,1)S(1)}, bf16[4,104]{1,0:T(4,128)(2,1)}, u32[]{:S(2)}) copy-start(bf16[4,104]{1,0:T(4,128)(2,1)} %param.14) | copy-start | bytes 2500
  8.9 17.9 %copy-start.20 = (u32[32]{0:T(128)S(1)}, u32[32]{0:T(128)}, u32[]{:S(2)}) copy-start(u32[32]{0:T(128)} %constant.187) | copy-start | bytes 388
  8.9 19.1 %copy-start.12 = (bf16[96]{0:T(256)(128)(2,1)S(1)}, bf16[96]{0:T(256)(128)(2,1)}, u32[]{:S(2)}) copy-start(bf16[96]{0:T(256)(128)(2,1)} %param.19) | copy-start | bytes 580
  8.9 19.1 %copy-start.13 = (bf16[104]{0:T(256)(128)(2,1)S(1)}, bf16[104]{0:T(256)(128)(2,1)}, u32[]{:S(2)}) copy-start(bf16[104]{0:T(256)(128)(2,1)} %param.15) | copy-start | bytes 628
  9.0 19.1 %copy-start.16 = (bf16[48]{0:T(256)(128)(2,1)S(1)}, bf16[48]{0:T(256)(128)(2,1)}, u32[]{:S(2)}) copy-start(bf16[48]{0:T(256)(128)(2,1)} %param.20) | copy-start | bytes 292
  9.9 57.1 %copy-start = (bf16[1,512,1536]{2,1,0:T(8,128)(2,1)S(1)}, bf16[1,512,1536]{2,1,0:T(8,128)(2,1)}, u32[]{:S(2)}) copy-start(bf16[1,512,1536]{2,1,0:T(8,128)(2,1)} %param.11) | copy-start | bytes 4718596
  26.6 43.3 %copy-start.5 = (bf16[1,512,1536]{2,1,0:T(8,128)(2,1)S(1)}, bf16[1,512,1536]{2,1,0:T(8,128)(2,1)}, u32[]{:S(2)}) copy-start(bf16[1,512,1536]{2,1,0:T(8,128)(2,1)} %param.21) | copy-start | bytes 4718596
  26.6 174.1 %all-gather.7.cloned.1.call-start = ((), (), s32[]{:S(2)}) async-start(), calls=%async_computation.5 | async-start | bytes 2654208 | tf_op jit(solution)/shard_map/all_gather | solution.py:528
  69.0 42.4 %collective-permute-start.1 = (bf16[512,1536]{1,0:T(8,128)(2,1)}, bf16[512,1536]{1,0:T(8,128)(2,1)}, u32[]{:S(2)}, u32[]{:S(2)}) collective-permute-start(bf16[512,1536]{1,0:T(8,128)(2,1)} %fusion.8), channel_id=1, source_target_pairs={{0,2},{1,3},{2,0},{3,1},{4,6},{5,7},{6,4},{7,5},{8,10},{9,11},{10,... | collective-permute-start | bytes 4718600 | tf_op jit(solution)/shard_map/ppermute | solution.py:423
  69.9 66.8 %collective-permute-start.4 = (bf16[512,1536]{1,0:T(8,128)(2,1)S(1)}, bf16[512,1536]{1,0:T(8,128)(2,1)}, u32[]{:S(2)}, u32[]{:S(2)}) collective-permute-start(bf16[512,1536]{1,0:T(8,128)(2,1)S(1)} %bitcast.189), channel_id=1, source_target_pairs={{0,2},{1,3},{2,0},{3,1},{4,6},{5,7},{6,4},{7,5},{8,10},{9,11},{10,... | collective-permute-start | bytes 4718600 | tf_op jit(solution)/shard_map/ppermute | solution.py:423
  71.0 65.7 %collective-permute-start = (bf16[512,1536]{1,0:T(8,128)(2,1)}, bf16[512,1536]{1,0:T(8,128)(2,1)}, u32[]{:S(2)}, u32[]{:S(2)}) collective-permute-start(bf16[512,1536]{1,0:T(8,128)(2,1)} %fusion.8), channel_id=1, source_target_pairs={{0,1},{1,0},{2,3},{3,2},{4,5},{5,4},{6,7},{7,6},{8,9},{9,8},{10,11... | collective-permute-start | bytes 4718600 | tf_op jit(solution)/shard_map/ppermute | solution.py:423
  71.0 71.1 %collective-permute-start.3 = (bf16[512,1536]{1,0:T(8,128)(2,1)S(1)}, bf16[512,1536]{1,0:T(8,128)(2,1)}, u32[]{:S(2)}, u32[]{:S(2)}) collective-permute-start(bf16[512,1536]{1,0:T(8,128)(2,1)S(1)} %bitcast.190), channel_id=1, source_target_pairs={{0,1},{1,0},{2,3},{3,2},{4,5},{5,4},{6,7},{7,6},{8,9},{9,8},{10,11... | collective-permute-start | bytes 4718600 | tf_op jit(solution)/shard_map/ppermute | solution.py:423
  71.5 20.6 %collective-permute-start.6 = (bf16[96,1536]{1,0:T(8,128)(2,1)}, bf16[96,1536]{1,0:T(8,128)(2,1)S(1)}, u32[]{:S(2)}, u32[]{:S(2)}) collective-permute-start(bf16[96,1536]{1,0:T(8,128)(2,1)} %param.13), channel_id=1, source_target_pairs={{0,0},{1,4},{2,8},{3,12},{4,16},{5,20},{6,24},{7,28},{8,1},{9,5},{... | collective-permute-start | bytes 884744 | tf_op jit(solution)/shard_map/ppermute | solution.py:525
  92.9 280.7 %reduce-scatter.5.cloned.1.call-start = ((), (), s32[]{:S(2)}) async-start(), calls=%async_computation.7 | async-start | bytes 2654208 | tf_op jit(solution)/shard_map/reduce_scatter | solution.py:621
  111.3 36.0 %collective-permute-start.2 = (bf16[512,1536]{1,0:T(8,128)(2,1)}, bf16[512,1536]{1,0:T(8,128)(2,1)S(1)}, u32[]{:S(2)}, u32[]{:S(2)}) collective-permute-start(bf16[512,1536]{1,0:T(8,128)(2,1)} %collective-permute-done.1), channel_id=1, source_target_pairs={{0,1},{1,0},{2,3},{3,2},{4,5},{5,4},{6,7},{7,6},{8,9},{9,8},{10,11... | collective-permute-start | bytes 4718600 | tf_op jit(solution)/shard_map/ppermute | solution.py:423
  136.7 12.0 %collective-permute-start.5 = (bf16[512,1536]{1,0:T(8,128)(2,1)}, bf16[512,1536]{1,0:T(8,128)(2,1)S(1)}, u32[]{:S(2)}, u32[]{:S(2)}) collective-permute-start(bf16[512,1536]{1,0:T(8,128)(2,1)} %collective-permute-done.4), channel_id=1, source_target_pairs={{0,1},{1,0},{2,3},{3,2},{4,5},{5,4},{6,7},{7,6},{8,9},{9,8},{10,11... | collective-permute-start | bytes 4718600 | tf_op jit(solution)/shard_map/ppermute | solution.py:423
  200.7 16.6 %copy-start.17 = (bf16[2048,768]{1,0:T(8,128)(2,1)S(1)}, bf16[2048,768]{1,0:T(8,128)(2,1)}, u32[]{:S(2)}) copy-start(bf16[2048,768]{1,0:T(8,128)(2,1)} %get-tuple-element.21) | copy-start | bytes 9437188
  211.5 1.4 collective-permute-start.7
  212.9 4.3 collective-permute-start.8
  226.7 191.4 %reduce-scatter.3.cloned.1.call-start = ((), (), s32[]{:S(2)}) async-start(), calls=%async_computation.6 | async-start | bytes 6635520 | tf_op jit(solution)/shard_map/reduce_scatter | solution.py:627
  319.4 33.8 %collective-permute-start.11 = (bf16[2,512,1536]{2,1,0:T(8,128)(2,1)}, bf16[2,512,1536]{2,1,0:T(8,128)(2,1)}, u32[]{:S(2)}, u32[]{:S(2)}) collective-permute-start(bf16[2,512,1536]{2,1,0:T(8,128)(2,1)} %fusion.19), channel_id=1, source_target_pairs={{0,1},{1,0},{2,3},{3,2},{4,5},{5,4},{6,7},{7,6},{8,9},{9,8},{10,11... | collective-permute-start | bytes 9437192 | tf_op jit(solution)/shard_map/ppermute | solution.py:423
  331.1 28.5 %collective-permute-start.9 = (bf16[2,512,1536]{2,1,0:T(8,128)(2,1)}, bf16[2,512,1536]{2,1,0:T(8,128)(2,1)}, u32[]{:S(2)}, u32[]{:S(2)}) collective-permute-start(bf16[2,512,1536]{2,1,0:T(8,128)(2,1)} %fusion.18), channel_id=1, source_target_pairs={{0,1},{1,0},{2,3},{3,2},{4,5},{5,4},{6,7},{7,6},{8,9},{9,8},{10,11... | collective-permute-start | bytes 9437192 | tf_op jit(solution)/shard_map/ppermute | solution.py:423
  333.5 4.5 collective-permute-start.14
  338.0 4.8 %collective-permute-start.15 = (f32[48,128]{1,0:T(8,128)S(1)}, f32[48,128]{1,0:T(8,128)S(1)}, u32[]{:S(2)}, u32[]{:S(2)}) collective-permute-start(f32[48,128]{1,0:T(8,128)S(1)} %fusion.54), channel_id=1, source_target_pairs={{0,8},{1,9},{2,10},{3,11},{4,12},{5,13},{6,14},{7,15},{8,0},{9,1},... | collective-permute-start | bytes 73736 | tf_op jit(solution)/shard_map/ppermute | solution.py:423
  342.8 6.6 %collective-permute-start.16 = (f32[48,128]{1,0:T(8,128)S(1)}, f32[48,128]{1,0:T(8,128)S(1)}, u32[]{:S(2)}, u32[]{:S(2)}) collective-permute-start(f32[48,128]{1,0:T(8,128)S(1)} %fusion.74), channel_id=1, source_target_pairs={{0,16},{1,17},{2,18},{3,19},{4,20},{5,21},{6,22},{7,23},{8,24},{9,... | collective-permute-start | bytes 73736 | tf_op jit(solution)/shard_map/ppermute | solution.py:423
  349.5 1.4 collective-permute-start.17
  350.9 18.9 %collective-permute-start.18 = (f32[4,48,128]{2,1,0:T(8,128)S(1)}, f32[4,48,128]{2,1,0:T(8,128)S(1)}, u32[]{:S(2)}, u32[]{:S(2)}) collective-permute-start(f32[4,48,128]{2,1,0:T(8,128)S(1)} %fusion.44), channel_id=1, source_target_pairs={{0,2},{1,3},{2,0},{3,1},{4,6},{5,7},{6,4},{7,5},{8,10},{9,11},{10,... | collective-permute-start | bytes 294920 | tf_op jit(solution)/shard_map/ppermute | solution.py:423
  359.6 41.4 %collective-permute-start.12 = (bf16[512,1536]{1,0:T(8,128)(2,1)}, bf16[512,1536]{1,0:T(8,128)(2,1)}, u32[]{:S(2)}, u32[]{:S(2)}) collective-permute-start(bf16[512,1536]{1,0:T(8,128)(2,1)} %fusion.25), channel_id=1, source_target_pairs={{0,2},{1,3},{2,0},{3,1},{4,6},{5,7},{6,4},{7,5},{8,10},{9,11},{10,... | collective-permute-start | bytes 4718600 | tf_op jit(solution)/shard_map/ppermute | solution.py:423
  368.9 65.8 %collective-permute-start.10 = (bf16[512,1536]{1,0:T(8,128)(2,1)}, bf16[512,1536]{1,0:T(8,128)(2,1)}, u32[]{:S(2)}, u32[]{:S(2)}) collective-permute-start(bf16[512,1536]{1,0:T(8,128)(2,1)} %fusion.24), channel_id=1, source_target_pairs={{0,2},{1,3},{2,0},{3,1},{4,6},{5,7},{6,4},{7,5},{8,10},{9,11},{10,... | collective-permute-start | bytes 4718600 | tf_op jit(solution)/shard_map/ppermute | solution.py:423
  373.5 66.9 %collective-permute-start.13 = (bf16[96,1536]{1,0:T(8,128)(2,1)}, bf16[96,1536]{1,0:T(8,128)(2,1)S(1)}, u32[]{:S(2)}, u32[]{:S(2)}) collective-permute-start(bf16[96,1536]{1,0:T(8,128)(2,1)} %reduce-scatter.5.cloned.1.call-done), channel_id=1, source_target_pairs={{0,0},{4,1},{8,2},{12,3},{16,4},{20,5},{24,6},{28,7},{1,8},{5,9},{... | collective-permute-start | bytes 884744 | tf_op jit(solution)/shard_map/ppermute | solution.py:624
  418.0 24.1 %all-to-all-start.1 = ((bf16[4,48,1920]{2,1,0:T(8,128)(2,1)}), bf16[4,48,1920]{2,1,0:T(8,128)(2,1)}, u32[]{:S(2)}, u32[]{:S(2)}) async-start(bf16[4,48,1920]{2,1,0:T(8,128)(2,1)} %bitcast.192), calls=%async_computation.2 | async-start | bytes 1474560 | tf_op jit(solution)/shard_map/all_to_all | solution.py:628
  (13 other events, 48.5 us)
Sparse Core Ops, SparseCore 0:
  26.8 110.7 all-gather.4
  140.3 51.5 all-gather.6
  226.8 71.6 reduce-scatter.4
  302.0 116.0 reduce-scatter.2

commit v2 on v1

--- a/solution.py
+++ b/solution.py
@@ -6,6 +6,7 @@
 from jax.experimental import pallas as pl
 from jax.experimental.pallas import tpu as pltpu
 from jax.sharding import PartitionSpec as P
+
 
 EPSILON = 1e-05
 HIGHEST = lax.Precision.HIGHEST
@@ -431,19 +432,6 @@
     return send(value, sizes, lambda b, s: (b, (s + 2 * k) % sizes[1]))
 
 
-def gather_pieces(piece, sizes):
-    ns = sizes[1]
-    me = lax.axis_index("seq")
-    place = lambda total, part, at: lax.dynamic_update_index_in_dim(total, part, at, 0)
-    total = jnp.zeros((ns,) + piece.shape, piece.dtype)
-    got = [piece] + [turn_row(piece, sizes, k) for k in range(1, ns // 2)]
-    for k, part in enumerate(got):
-        at = (me + ns - 2 * k) % ns
-        total = place(total, part, at)
-        total = place(total, swap_core(part, sizes), at ^ 1)
-    return total
-
-
 def scatter_pieces(value, sizes):
     ns = sizes[1]
     me = lax.axis_index("seq")
@@ -455,7 +443,8 @@
     total = lax.dynamic_index_in_dim(both, chip, 0, False)
     for k in range(1, ns // 2):
         part = lax.dynamic_index_in_dim(both, (chip + k) % (ns // 2), 0, False)
-        total = total + turn_row(part.astype(BF16), sizes, k).astype(F32)
+        part = turn_row(part.astype(BF16), sizes, k)
+        total = total + part.astype(F32)
     return total
 
 
@@ -464,20 +453,111 @@
     while k < sizes[axis]:
         step = k
         if axis == 0:
-            value = value + send(value, sizes, lambda b, s: (b ^ step, s))
+            other = send(value, sizes, lambda b, s: (b ^ step, s))
         else:
-            value = value + send(value, sizes, lambda b, s: (b, s ^ step))
+            other = send(value, sizes, lambda b, s: (b, s ^ step))
+        value = value + other
         k *= 2
     return value
 
 
-def collect_over_seq(value, sizes):
+def sum_depth(value, sizes):
+    deep = sizes[0] // 2
+    z = lax.axis_index("batch") // 2
+    got = [value]
+    for k in range(1, deep):
+        got.append(turn_deep(value, sizes, k))
+    got = jnp.stack(got)
+    at = lambda d: lax.dynamic_index_in_dim(got, (z + deep - d) % deep, 0, False)
+    return functools.reduce(jnp.add, [at(d) for d in range(deep)])
+
+
+def sum_seq(value, sizes):
+    total = value
+    for k in range(1, sizes[1]):
+        other = turn_seq(value, sizes, k)
+        total = total + other
+    return total
+
+
+def collect(value, index, count, sizes, axes):
+    total = lax.dynamic_update_index_in_dim(
+        jnp.zeros((count,) + value.shape, value.dtype), value, index, 0
+    )
+    for axis in axes:
+        total = add_over(total, sizes, axis)
+    return total
+
+
+def after(value, other):
+    return lax.optimization_barrier((value, other))[0]
+
+
+def swap_side(value, sizes):
+    return send(value, sizes, lambda b, s: (b ^ 1, s))
+
+
+def turn_deep(value, sizes, k):
+    deep = sizes[0] // 2
+    return send(value, sizes, lambda b, s: ((b // 2 + k) % deep * 2 + b % 2, s))
+
+
+def turn_seq(value, sizes, k):
+    return send(value, sizes, lambda b, s: (b, (s + k) % sizes[1]))
+
+
+def exchange_seq(blocks, sizes):
     ns = sizes[1]
     me = lax.axis_index("seq")
     total = lax.dynamic_update_index_in_dim(
-        jnp.zeros((ns,) + value.shape, value.dtype), value, me, 0
-    )
-    return add_over(total, sizes, 1)
+        jnp.zeros_like(blocks), lax.dynamic_index_in_dim(blocks, me, 0, False), me, 0
+    )
+    for k in range(1, ns):
+        part = lax.dynamic_index_in_dim(blocks, (me + k) % ns, 0, False)
+        got = turn_seq(part, sizes, k)
+        total = lax.dynamic_update_index_in_dim(total, got, (me + ns - k) % ns, 0)
+    return total
+
+
+def gather_batch(block, sizes):
+    deep = sizes[0] // 2
+    me = lax.axis_index("batch")
+    z, x = me // 2, me % 2
+    total = jnp.zeros((deep * 2,) + block.shape, block.dtype)
+    place = lambda part, at: lax.dynamic_update_index_in_dim(total, part, at, 0)
+    here = block
+    for k in range(deep):
+        there = swap_side(here, sizes)
+        at = (z + deep - k) % deep * 2
+        total = place(here, at + x)
+        if k < deep - 1:
+            here = turn_deep(here, sizes, 1)
+        total = place(there, at + 1 - x)
+    return total.reshape((-1,) + block.shape[1:]), here
+
+
+def sides(blocks, sizes):
+    x = lax.axis_index("batch") % 2
+    split = blocks.reshape((sizes[0] // 2, 2) + blocks.shape[1:])
+    pick = lambda side: lax.dynamic_index_in_dim(split, side, 1, False)
+    return pick(1 - x), pick(x)
+
+
+def scatter_batch(blocks, sizes):
+    deep = sizes[0] // 2
+    z = lax.axis_index("batch") // 2
+    give, keep = sides(blocks, sizes)
+    pick = lambda value, at: lax.dynamic_index_in_dim(value, at % deep, 0, False)
+    total = None
+    for k in range(1, deep + 1):
+        at = z + deep - k
+        other = swap_side(pick(give, at), sizes)
+        both = pick(keep, at).astype(F32) + other.astype(F32)
+        total = both if total is None else total + both
+        if k < deep:
+            total = turn_deep(total.astype(BF16), sizes, 1)
+            total = total.astype(F32)
+    return total
 
 
 def per_device(
@@ -503,6 +583,11 @@
     per_seq = piece * ns // L
 
     dt_at = inner + conv_channels
+    small = jnp.concatenate([conv_weight.reshape(-1), conv_bias, gated_gain])
+    small_count = small.shape[0]
+    small_lanes = -(-small_count // in_rows)
+    small = jnp.pad(small, (0, small_lanes * in_rows - small_count)).reshape(in_rows, small_lanes)
+    spare = LANES - own_heads - small_lanes
     payload = jnp.stack(
         [
             jnp.concatenate(
@@ -510,28 +595,26 @@
                     in_proj[:, s * width : (s + 1) * width],
                     in_proj[:, inner + s * width : inner + (s + 1) * width],
                     in_proj[:, 2 * inner : dt_at],
-                    jnp.pad(
-                        in_proj[:, dt_at + s * own_heads : dt_at + (s + 1) * own_heads],
-                        ((0, 0), (0, LANES - own_heads)),
-                    ),
+                    in_proj[:, dt_at + s * own_heads : dt_at + (s + 1) * own_heads],
+                    small,
+                    jnp.zeros((in_rows, spare), BF16),
                 ],
                 axis=1,
             )
             for s in range(ns)
         ]
     )
-    mine = lax.all_to_all(payload, "seq", 0, 0, tiled=False).reshape(ns * in_rows, columns)
-    weight_in = lax.all_gather(mine, "batch", axis=0, tiled=True)
+    gains = after(jnp.pad(norm_gain.astype(F32), (0, -in_rows % LANES)), payload)
+    gains = collect(gains, me_b * ns + me_s, devices, sizes, (0, 1))
+    norm_all = gains[:, :in_rows].reshape(1, model)
+    mine = exchange_seq(payload, sizes).reshape(ns * in_rows, columns)
+    weight_in, last_in = gather_batch(mine, sizes)
     out_rows = lax.ppermute(
-        out_proj, AXES, [(j, (j % nb) * ns + j // nb) for j in range(devices)]
-    )
-    weight_out = lax.all_gather(out_rows, "batch", axis=0, tiled=True)
-
-    small = jnp.concatenate(
-        [conv_weight.reshape(-1), conv_bias.reshape(-1), gated_gain, norm_gain]
-    ).reshape(1, -1)
-    small = lax.all_gather(small, "seq", axis=0, tiled=True)
-    small = lax.all_gather(small, "batch", axis=0, tiled=True).astype(F32)
+        after(out_proj, mine), AXES, [(j, (j % nb) * ns + j // nb) for j in range(devices)]
+    )
+
+    at = width + channels + own_heads
+    small = weight_in[:, at : at + small_lanes].astype(F32).reshape(devices, -1)
     conv_all = jnp.moveaxis(
         small[:, : taps * conv_part].reshape(devices, taps, conv_part), 0, 1
     ).reshape(taps, conv_channels)
@@ -539,8 +622,6 @@
     bias_all = small[:, at : at + conv_part].reshape(1, conv_channels)
     at += conv_part
     gain_all = small[:, at : at + gated_gain.shape[0]].reshape(1, inner)
-    at += gated_gain.shape[0]
-    norm_all = small[:, at:].reshape(1, model)
     conv_all = jnp.concatenate([conv_all, bias_all], axis=0)
     conv_rows = rows_of(
         [
@@ -567,10 +648,6 @@
         jnp.arange(width)[:, None] // head_size == jnp.arange(LANES)[None, :]
     ).astype(BF16)
 
-    stream = hidden.reshape(-1, model).astype(F32)
-    spread = lax.rsqrt(jnp.mean(stream * stream, axis=-1, keepdims=True) + EPSILON)
-    normed = (stream * spread * norm_all).astype(BF16)
-
     def in_order(pieces):
         value = pieces.reshape((ns, seq_count, piece, model))
         return jnp.swapaxes(value, 0, 1).reshape(tokens, model)
@@ -579,13 +656,20 @@
         value = value.reshape((seq_count, ns, piece, model))
         return jnp.swapaxes(value, 0, 1).reshape(ns, seq_count * piece, model)
 
-    normed_all = in_order(gather_pieces(normed, sizes))
-    upstream = in_order(gather_pieces(cotangent.reshape(-1, model), sizes))
+    low = hidden.reshape(-1, model)
+    grad_low = cotangent.reshape(-1, model)
+    hidden_all = after(in_order(lax.all_gather(low, "seq")), last_in).astype(F32)
+    spread = lax.rsqrt(jnp.mean(hidden_all * hidden_all, axis=-1, keepdims=True) + EPSILON)
+    normed_all = (hidden_all * spread * norm_all).astype(BF16)
+    upstream = lax.all_gather(after(grad_low, payload), "seq")
+    upstream = in_order(upstream)
+    weight_out = lax.all_gather(out_rows, "batch", axis=0, tiled=True)
 
     projected = jnp.dot(normed_all, weight_in, preferred_element_type=F32)
     convolved, y, ungained, squares, entering = forward_scan(
         projected, conv_rows, head_rows, lane_rows, width, state, taps, per_seq
     )
+    weight_out = after(weight_out, ungained)
     grad_gated = jnp.einsum("td,kd->tk", upstream, weight_out, preferred_element_type=F32)
     sums = jnp.stack(
         [
@@ -593,7 +677,7 @@
             jnp.sum(grad_gated * ungained.astype(F32), axis=1),
         ]
     )
-    sums = add_over(sums, sizes, 1)
+    sums = sum_seq(sums, sizes)
     inverse = lax.rsqrt(sums[0] / inner + EPSILON)
     pull = inverse * inverse * inverse * sums[1] / inner
     stats = jnp.stack([inverse, pull], axis=1)
@@ -602,21 +686,28 @@
     own_inverse = lax.dynamic_index_in_dim(
         jnp.swapaxes(inverse.reshape(seq_count, ns, piece), 0, 1), me_s, 0, False
     ).reshape(-1, 1)
+    stream = low.astype(F32)
     result = (stream + own_inverse * out_sum).astype(BF16)
     gated_low = (ungained.astype(F32) * inverse[:, None]).astype(BF16)
     grad_out_w = jnp.einsum("tk,td->kd", gated_low, upstream, preferred_element_type=F32)
 
     grad_proj, conv_acc, lane_acc, head_acc = backward_scan(
-        projected, convolved, y, entering, grad_gated, stats, conv_rows, head_rows, lane_rows,
+        projected, convolved, y, entering, grad_gated, after(stats, grad_out_w), conv_rows, head_rows, lane_rows,
         expand, width, state, taps, per_seq,
     )
-    grad_in_w = jnp.einsum("td,tk->dk", normed_all, grad_proj, preferred_element_type=F32)
-    grad_normed = jnp.einsum("tk,dk->td", grad_proj, weight_in, preferred_element_type=F32)
-    grad_normed = scatter_pieces(in_pieces(grad_normed), sizes)
-    scaled = grad_normed * norm_all
-    unit = stream * spread
-    grad_stream = spread * (scaled - unit * jnp.mean(scaled * unit, axis=-1, keepdims=True))
-    hidden_grad = (cotangent.reshape(-1, model).astype(F32) + grad_stream).astype(BF16)
+    cut = (columns // 2 + LANES - 1) // LANES * LANES
+    grad_in_w = []
+    for name, lo, hi in (("a", 0, cut), ("b", cut, columns)):
+        part = jnp.einsum("td,tk->dk", normed_all, grad_proj[:, lo:hi], preferred_element_type=F32)
+        grad_in_w.append((name, part.astype(BF16).reshape(nb, ns * in_rows, hi - lo)))
+    scaled = jnp.einsum("tk,dk->td", grad_proj, weight_in, preferred_element_type=F32)
+    scaled = lax.psum_scatter(
+        in_pieces(scaled.astype(BF16)), "seq", scatter_dimension=0, tiled=False
+    ).astype(F32) * norm_all
+    own_spread = lax.rsqrt(jnp.mean(stream * stream, axis=-1, keepdims=True) + EPSILON)
+    unit = stream * own_spread
+    grad_stream = own_spread * (scaled - unit * jnp.mean(scaled * unit, axis=-1, keepdims=True))
+    hidden_grad = (grad_low.astype(F32) + grad_stream).astype(BF16)
 
     out_part = lax.psum_scatter(
         grad_out_w.astype(BF16), "batch", scatter_dimension=0, tiled=True
@@ -624,10 +715,11 @@
     out_proj_grad = lax.ppermute(
         out_part, AXES, [((j % nb) * ns + j // nb, j) for j in range(devices)]
     ).astype(F32)
-    in_part = lax.psum_scatter(grad_in_w.astype(BF16), "batch", scatter_dimension=0, tiled=True)
-    by_source = lax.all_to_all(
-        in_part.reshape(ns, in_rows, columns), "seq", 0, 0, tiled=False
-    ).astype(F32)
+    by_source = []
+    for name, part in grad_in_w:
+        part = scatter_batch(part, sizes).astype(BF16)
+        by_source.append(exchange_seq(part.reshape(ns, in_rows, -1), sizes))
+    by_source = jnp.concatenate(by_source, axis=2).astype(F32)
     across = lambda lo, hi: jnp.concatenate([by_source[s, :, lo:hi] for s in range(ns)], axis=1)
     in_proj_grad = jnp.concatenate(
         [
@@ -651,7 +743,11 @@
         ]
     )
     packed = jnp.pad(packed, (0, -packed.shape[0] % (8 * LANES))).reshape(-1, LANES)
-    packed = collect_over_seq(add_over(packed, sizes, 0), sizes).reshape(ns, -1)
+    other = swap_side(packed, sizes)
+    packed = packed + other
+    packed = sum_depth(packed, sizes)
+    packed = collect(packed, me_s, ns, sizes, (1,))
+    packed = packed.reshape(ns, -1)
     rows = (taps + 1) * channels
     conv_grads = packed[:, :rows].reshape(ns, taps + 1, channels)
     conv_grads = jnp.concatenate(
@@ -714,10 +810,10 @@
         both,
     )
     sizes = (mesh.shape["batch"], mesh.shape["seq"])
+
+    def step(*args):
+        return per_device(sizes, *args)
+
     return jax.shard_map(
-        functools.partial(per_device, sizes),
-        mesh=mesh,
-        in_specs=in_specs,
-        out_specs=out_specs,
-        check_vma=False,
-    )
+        step, mesh=mesh, in_specs=in_specs, out_specs=out_specs, check_vma=False
+    )

time: 453 us -> 505 us (1.11)
  waiting for transfers between devices: 110 us -> 178 us
  blocking collectives: 53.6 us -> 0 us
  starting transfers between devices: 23 us -> 70.8 us
  local copies, waits for them, and re-layouts: 61.6 us -> 36.1 us
  matrix products: 80.9 us -> 87 us
  other arithmetic: 31.8 us -> 37.6 us
    ppermute x17 -> x46, waiting for transfers between devices: 94.9 us -> 177 us  [send(): return lax.ppermute(value, AXES, pairs)]
    ppermute x17 -> x46, starting transfers between devices: 15 us -> 68 us  [send(): return lax.ppermute(value, AXES, pairs)]
    all_gather x1 -> x0, blocking collectives: 32.5 us -> none  [per_device(): small = lax.all_gather(small, 'batch', axis=0, tiled=True).astype(F32)]
    all_to_all x1 -> x0, blocking collectives: 15.3 us -> none  [per_device(): lax.all_to_all(payload, 'seq', 0, 0, tiled=False)]
    reduce_scatter x1, waiting for transfers between devices: 13.8 us -> 0.01 us  [per_device(): lax.psum_scatter(in_pieces(scaled.astype(BF16)), 'seq', scatter_dimension...]
    dynamic_update_slice x7 -> x18, local copies, waits for them, and re-layouts: 14.6 us -> 2.02 us  [the longest x8 1.83 us: gather_batch(): place = lambda part, at: lax.dynamic_update_index_in_dim(total, part, at, 0)]
    convert_element_type x2 -> x10, other arithmetic: 2.79 us -> 14.5 us  [the longest x6 9.64 us: scatter_batch(): total = turn_deep(total.astype(BF16), sizes, 1)]
    another operation x3 -> x1, local copies, waits for them, and re-layouts: 7.66 us -> 0.01 us
  transfers between devices with their start and end apart: 24 -> 53, of which waited for: 11 -> 25; matrix products, arithmetic and copies ran while one was open for 30% -> 25% of each run, Pallas kernels for 17% -> 15%
where the time goes in v2:
time: 505 us; the launch traced here: 501 us
  waiting for transfers between devices  178 us (35%)
  matrix products  87 us (17%)
  Pallas kernels  76.4 us (15%)
  starting transfers between devices  70.8 us (14%)
  other arithmetic  37.6 us (7%)
  local copies, waits for them, and re-layouts  36.1 us (7%)
  between operations  14.9 us (3%)
    ppermute x46, waiting for transfers between devices, send(): return lax.ppermute(value, AXES, pairs)  177 us
    ppermute x46, starting transfers between devices, send(): return lax.ppermute(value, AXES, pairs)  68 us
    pallas_call x1, Pallas kernels, backward_scan(): pl.pallas_call(functools.partial(backward_body, width, state, taps, per_s...  46.5 us
    pallas_call x1, Pallas kernels, forward_scan(): pl.pallas_call(functools.partial(forward_body, width, state, taps, per_se...  29.9 us
    dot_general x2, matrix products, per_device(): jnp.einsum('td,tk->dk', normed_all, grad_proj[:, lo:hi], preferred_elemen...  20.3 us
    dot_general x1, matrix products, per_device(): jnp.einsum('tk,dk->td', grad_proj, weight_in, preferred_element_type=F32)  18.5 us
    dot_general x1, matrix products, per_device(): projected = jnp.dot(normed_all, weight_in, preferred_element_type=F32)  17.9 us
    dot_general x1, matrix products, per_device(): jnp.einsum('td,kd->tk', upstream, weight_out, preferred_element_type=F32)  10.3 us
  transfers between devices with their start and end apart: 53, of which 25 were waited for; matrix products, arithmetic and copies ran while one was open for 25% of the time, Pallas kernels for 15%

profile of v2, /device:TPU:0, one launch (start us, length us, event | category | flops | bytes accessed | tf_op | source)
XLA Modules:
  0.0 501.0 jit_solution(7581278899544553954)
XLA Ops:
  20.6 11.7 %collective-permute-done.1 = bf16[48,1920]{1,0:T(8,128)(2,1)S(1)} collective-permute-done((bf16[48,1920]{1,0:T(8,128)(2,1)S(1)}, bf16[48,1920]{1,0:T(8,128)(2,1)S(1)}, u32[]{:S(2)}, u32[]{:S(2)}) %collective-permute-start.1) | collective-permute-done | bytes 184352 | tf_op jit(solution)/shard_map/ppermute | solution.py:424
  34.0 13.2 %collective-permute-start.6 = (f32[32,128]{1,0:T(8,128)S(1)}, f32[32,128]{1,0:T(8,128)S(1)}, u32[]{:S(2)}, u32[]{:S(2)}) collective-permute-start(f32[32,128]{1,0:T(8,128)S(1)} %dynamic_update_slice.80), channel_id=1, source_target_pairs={{0,4},{1,5},{2,6},{3,7},{4,0},{5,1},{6,2},{7,3},{8,12},{9,13},{10,... | collective-permute-start | bytes 49160 | tf_op jit(solution)/shard_map/ppermute | solution.py:424
  48.9 9.6 %collective-permute-start.7 = (f32[32,128]{1,0:T(8,128)S(1)}, f32[32,128]{1,0:T(8,128)S(1)}, u32[]{:S(2)}, u32[]{:S(2)}) collective-permute-start(f32[32,128]{1,0:T(8,128)S(1)} %add.566), channel_id=1, source_target_pairs={{0,8},{1,9},{2,10},{3,11},{4,12},{5,13},{6,14},{7,15},{8,0},{9,1},... | collective-permute-start | bytes 49160 | tf_op jit(solution)/shard_map/ppermute | solution.py:424
  66.3 5.8 %collective-permute-start.10 = (f32[32,128]{1,0:T(8,128)S(1)}, f32[32,128]{1,0:T(8,128)S(1)}, u32[]{:S(2)}, u32[]{:S(2)}) collective-permute-start(f32[32,128]{1,0:T(8,128)S(1)} %add.569), channel_id=1, source_target_pairs={{0,2},{1,3},{2,0},{3,1},{4,6},{5,7},{6,4},{7,5},{8,10},{9,11},{10,... | collective-permute-start | bytes 49160 | tf_op jit(solution)/shard_map/ppermute | solution.py:424
  74.8 7.1 %collective-permute-done.3 = bf16[192,1920]{1,0:T(8,128)(2,1)S(1)} collective-permute-done((bf16[192,1920]{1,0:T(8,128)(2,1)S(1)}, bf16[192,1920]{1,0:T(8,128)(2,1)S(1)}, u32[]{:S(2)}, u32[]{:S(2)}) %collective-permute-start.3) | collective-permute-done | bytes 737312 | tf_op jit(solution)/shard_map/ppermute | solution.py:424
  84.4 26.5 %collective-permute-done.4 = bf16[192,1920]{1,0:T(8,128)(2,1)S(1)} collective-permute-done((bf16[192,1920]{1,0:T(8,128)(2,1)S(1)}, bf16[192,1920]{1,0:T(8,128)(2,1)S(1)}, u32[]{:S(2)}, u32[]{:S(2)}) %collective-permute-start.4) | collective-permute-done | bytes 737312 | tf_op jit(solution)/shard_map/ppermute | solution.py:424
  113.1 30.2 %collective-permute-done.5 = bf16[192,1920]{1,0:T(8,128)(2,1)S(1)} collective-permute-done((bf16[192,1920]{1,0:T(8,128)(2,1)S(1)}, bf16[192,1920]{1,0:T(8,128)(2,1)S(1)}, u32[]{:S(2)}, u32[]{:S(2)}) %collective-permute-start.5) | collective-permute-done | bytes 737312 | tf_op jit(solution)/shard_map/ppermute | solution.py:424
  143.2 2.8 collective-permute-start.14
  146.2 14.2 %collective-permute-done.14 = bf16[192,1920]{1,0:T(8,128)(2,1)S(1)} collective-permute-done((bf16[192,1920]{1,0:T(8,128)(2,1)S(1)}, bf16[192,1920]{1,0:T(8,128)(2,1)S(1)}, u32[]{:S(2)}, u32[]{:S(2)}) %collective-permute-start.14) | collective-permute-done | bytes 737312 | tf_op jit(solution)/shard_map/ppermute | solution.py:424
  165.5 4.2 fusion
  170.0 17.9 %fusion.70.p_ref = f32[2048,1920]{1,0:T(8,128)} fusion(bf16[1536,1920]{1,0:T(8,128)(2,1)S(1)} %bitcast.234, bf16[2048,1536]{1,0:T(8,128)(2,1)} %bitcast.236, f32[1536]{0:T(1024)S(1)} %mul.158, f32[2048]{0:T(1024)S(1)} %add_rsqrt_fusion), kind=kOutput, calls=%fused_computation.184 | convolution fusion | flops 12092178432 | bytes 27932672 | tf_op jit(solution)/shard_map/dot_general | solution.py:668
  187.9 29.9 %forward_scan.1 = (f32[2048,1024]{1,0:T(8,128)}, f32[2048,768]{1,0:T(8,128)}, bf16[2048,768]{1,0:T(8,128)(2,1)}, f32[2048,128]{1,0:T(8,128)}, f32[2048,768]{1,0:T(8,128)}) custom-call(f32[2048,1920]{1,0:T(8,128)} %fusion.70.p_ref, f32[8,1024]{1,0:T(8,128)} %pad.33.conv_ref, f32[8,128]{1,0:T(8,128)} %pad.36.head_ref, f32[8,768]{1,0:T(8,128)} %select_maximum_fusion.1.lane_ref), custom_call_target="tpu_custom_call" | custom-call | flops 1610612736 | bytes 39321600 | tf_op jit(solution)/shard_map/forward_scan/pallas_call | solution.py:325
  219.5 10.3 %fusion.3 = (f32[2048]{0:T(1024)S(1)}, f32[2048,768]{1,0:T(8,128)}) fusion(bf16[2048,768]{1,0:T(8,128)(2,1)} %get-tuple-element.31, bf16[2048,1536]{1,0:T(8,128)(2,1)} %all-gather.9.cloned.1.call-done, bf16[768,1536]{1,0:T(8,128)(2,1)} %all-gather.7.cloned.1.call-done), kind=kOutput, calls=%fused_computation.8 | convolution fusion | flops 4836554752 | bytes 18096128 | tf_op jit(solution)/shard_map/td,kd->tk/dot_general | solution.py:673
  230.5 3.2 collective-permute-done.17
  233.7 9.8 %fusion.29 = bf16[768,1536]{1,0:T(8,128)(2,1)} fusion(bf16[2048,1536]{1,0:T(8,128)(2,1)} %all-gather.9.cloned.1.call-done, bf16[2048,768]{1,0:T(8,128)(2,1)} %get-tuple-element.31, f32[2048]{0:T(1024)S(1)} %bitcast.269), kind=kOutput, calls=%fused_computation.36 | convolution fusion | flops 4836556800 | bytes 11804672 | tf_op jit(solution)/shard_map/tk,td->kd/dot_general | solution.py:692
  243.7 10.0 %fusion.76 = f32[2048,1536]{1,0:T(8,128)} fusion(bf16[2048,768]{1,0:T(8,128)(2,1)} %get-tuple-element.31, bf16[768,1536]{1,0:T(8,128)(2,1)} %all-gather.7.cloned.1.call-done), kind=kOutput, calls=%fused_computation.188 | convolution fusion | flops 4831838208 | bytes 18087936 | tf_op jit(solution)/shard_map/dot_general | solution.py:684
  255.1 46.5 %backward_scan.1 = (bf16[2048,1920]{1,0:T(8,128)(2,1)}, f32[8,1024]{1,0:T(8,128)}, f32[8,768]{1,0:T(8,128)}, f32[8,128]{1,0:T(8,128)}) custom-call(f32[2048,1920]{1,0:T(8,128)} %fusion.70.p_ref, f32[2048,1024]{1,0:T(8,128)} %get-tuple-element.33.v_ref, f32[2048,768]{1,0:T(8,128)} %get-tuple-element.34.y_ref, f32[2048,768]{1,0:T(8,128)} %get-tuple-element.35.enter_ref, ...), custom_call_target="tpu_custom_call" | custom-call | flops 4831838208 | bytes 55050240 | tf_op jit(solution)/shard_map/backward_scan/pallas_call | solution.py:368
  301.7 18.5 %convolution_convert_fusion = bf16[2048,1536]{1,0:T(8,128)(2,1)} fusion(bf16[2048,1920]{1,0:T(8,128)(2,1)} %get-tuple-element.37, bf16[1536,1920]{1,0:T(8,128)(2,1)} %bitcast.233), kind=kOutput, calls=%fused_computation.7 | convolution fusion | flops 12082741248 | bytes 20054016 | tf_op jit(solution)/shard_map/tk,dk->td/dot_general | solution.py:703
  320.2 4.9 fusion.28
  328.9 12.5 %fusion.15 = bf16[1536,896]{1,0:T(8,128)(2,1)S(1)} fusion(bf16[2048,1920]{1,0:T(8,128)(2,1)} %get-tuple-element.37, bf16[2048,1536]{1,0:T(8,128)(2,1)} %bitcast.237, f32[1536]{0:T(1024)S(1)} %mul.158, f32[2048]{0:T(1024)S(1)} %add_rsqrt_fusion), kind=kOutput, calls=%fused_computation.24 | convolution fusion | flops 5651103744 | bytes 12728320 | tf_op jit(solution)/shard_map/td,tk->dk/dot_general | solution.py:701
  343.5 7.8 %fusion.10 = bf16[1536,1024]{1,0:T(8,128)(2,1)S(1)} fusion(bf16[2048,1920]{1,0:T(8,128)(2,1)S(1)} %bitcast.280, bf16[2048,1536]{1,0:T(8,128)(2,1)S(1)} %bitcast.240, f32[1536]{0:T(1024)S(1)} %mul.158, f32[2048]{0:T(1024)S(1)} %add_rsqrt_fusion), kind=kOutput, calls=%fused_computation.21 | convolution fusion | flops 6456606720 | bytes 13647872 | tf_op jit(solution)/shard_map/td,tk->dk/dot_general | solution.py:701
  368.9 4.6 collective-permute-done.47
  373.7 5.4 %collective-permute-done.33 = bf16[192,896]{1,0:T(8,128)(2,1)} collective-permute-done((bf16[192,896]{1,0:T(8,128)(2,1)}, bf16[192,896]{1,0:T(8,128)(2,1)}, u32[]{:S(2)}, u32[]{:S(2)}) %collective-permute-start.33) | collective-permute-done | bytes 344096 | tf_op jit(solution)/shard_map/ppermute | solution.py:424
  381.1 3.7 collective-permute-done.32
  391.0 7.9 %collective-permute-done.34 = bf16[192,896]{1,0:T(8,128)(2,1)S(1)} collective-permute-done((bf16[192,896]{1,0:T(8,128)(2,1)S(1)}, bf16[192,896]{1,0:T(8,128)(2,1)S(1)}, u32[]{:S(2)}, u32[]{:S(2)}) %collective-permute-start.34) | collective-permute-done | bytes 344096 | tf_op jit(solution)/shard_map/ppermute | solution.py:424
  402.6 4.8 collective-permute-done.22
  417.0 3.6 collective-permute-done.24
  423.2 4.2 collective-permute-done.39
  427.4 4.9 collective-permute-done.26
  437.7 4.9 bitcast_add_fusion
  454.0 32.8 %collective-permute-done.20 = bf16[512,1536]{1,0:T(8,128)(2,1)} collective-permute-done((bf16[512,1536]{1,0:T(8,128)(2,1)}, bf16[512,1536]{1,0:T(8,128)(2,1)}, u32[]{:S(2)}, u32[]{:S(2)}) %collective-permute-start.20) | collective-permute-done | bytes 1572896 | tf_op jit(solution)/shard_map/ppermute | solution.py:424
  486.8 5.2 %fusion.24 = (f32[512]{0:T(512)S(1)}, bf16[1,512,1536]{2,1,0:T(8,128)(2,1)}) fusion(bf16[1,512,1536]{2,1,0:T(8,128)(2,1)} %reduce-scatter.3.cloned.1.call-done, bf16[1,512,1536]{2,1,0:T(8,128)(2,1)S(1)} %copy-done, f32[512]{0:T(512)S(1)} %add_rsqrt_fusion.1, f32[1536]{0:T(1024)S(1)} %mul.158, bf16[512,1536]{1,0:T(8,128)(2,1)} %collective-permute-done.20, ...), kind=kLoop, calls=%fused_computation.31 | loop fusion | flops 8650240 | bytes 9449476 | tf_op jit(solution)/shard_map/reduce_sum | solution.py:709
  (266 shorter events, 107.2 us)
Async XLA Ops:
  7.2 158.3 %all-gather.5.cloned.1.call-start = ((), (), s32[]{:S(2)}) async-start(), calls=%async_computation.2 | async-start | bytes 7864320 | tf_op jit(solution)/shard_map/all_gather | solution.py:661
  8.0 211.5 %all-gather.7.cloned.1.call-start = ((), (), s32[]{:S(2)}) async-start(), calls=%async_computation.3 | async-start | bytes 2654208 | tf_op jit(solution)/shard_map/all_gather | solution.py:666
  15.4 16.9 %collective-permute-start.2 = (bf16[48,1920]{1,0:T(8,128)(2,1)S(1)}, bf16[48,1920]{1,0:T(8,128)(2,1)S(1)}, u32[]{:S(2)}, u32[]{:S(2)}) collective-permute-start(bf16[48,1920]{1,0:T(8,128)(2,1)S(1)} %get-tuple-element.69), channel_id=1, source_target_pairs={{0,3},{1,0},{2,1},{3,2},{4,7},{5,4},{6,5},{7,6},{8,11},{9,8},{10,9... | collective-permute-start | bytes 552968 | tf_op jit(solution)/shard_map/ppermute | solution.py:424
  17.4 14.9 %collective-permute-start.1 = (bf16[48,1920]{1,0:T(8,128)(2,1)S(1)}, bf16[48,1920]{1,0:T(8,128)(2,1)S(1)}, u32[]{:S(2)}, u32[]{:S(2)}) collective-permute-start(bf16[48,1920]{1,0:T(8,128)(2,1)S(1)} %get-tuple-element.70), channel_id=1, source_target_pairs={{0,2},{1,3},{2,0},{3,1},{4,6},{5,7},{6,4},{7,5},{8,10},{9,11},{10,... | collective-permute-start | bytes 552968 | tf_op jit(solution)/shard_map/ppermute | solution.py:424
  33.9 185.6 %all-gather.9.cloned.1.call-start = ((), (), s32[]{:S(2)}) async-start(), calls=%async_computation.6 | async-start | bytes 7864320 | tf_op jit(solution)/shard_map/all_gather | solution.py:664
  34.0 14.9 %collective-permute-start.6 = (f32[32,128]{1,0:T(8,128)S(1)}, f32[32,128]{1,0:T(8,128)S(1)}, u32[]{:S(2)}, u32[]{:S(2)}) collective-permute-start(f32[32,128]{1,0:T(8,128)S(1)} %dynamic_update_slice.80), channel_id=1, source_target_pairs={{0,4},{1,5},{2,6},{3,7},{4,0},{5,1},{6,2},{7,3},{8,12},{9,13},{10,... | collective-permute-start | bytes 49160 | tf_op jit(solution)/shard_map/ppermute | solution.py:424
  47.2 402.0 %reduce-scatter.5.cloned.1.call-start = ((), (), s32[]{:S(2)}) async-start(), calls=%async_computation.5 | async-start | bytes 2654208 | tf_op jit(solution)/shard_map/reduce_scatter | solution.py:712
  60.3 22.8 %collective-permute-start.11 = (bf16[192,1920]{1,0:T(8,128)(2,1)S(1)}, bf16[192,1920]{1,0:T(8,128)(2,1)}, u32[]{:S(2)}, u32[]{:S(2)}) collective-permute-start(bf16[192,1920]{1,0:T(8,128)(2,1)S(1)} %bitcast.248), channel_id=1, source_target_pairs={{0,4},{1,5},{2,6},{3,7},{4,0},{5,1},{6,2},{7,3},{8,12},{9,13},{10,... | collective-permute-start | bytes 2211848 | tf_op jit(solution)/shard_map/ppermute | solution.py:424
  61.9 20.0 %collective-permute-start.3 = (bf16[192,1920]{1,0:T(8,128)(2,1)S(1)}, bf16[192,1920]{1,0:T(8,128)(2,1)S(1)}, u32[]{:S(2)}, u32[]{:S(2)}) collective-permute-start(bf16[192,1920]{1,0:T(8,128)(2,1)S(1)} %bitcast.249), channel_id=1, source_target_pairs={{0,8},{1,9},{2,10},{3,11},{4,12},{5,13},{6,14},{7,15},{8,16},{9,17... | collective-permute-start | bytes 2211848 | tf_op jit(solution)/shard_map/ppermute | solution.py:424
  81.9 30.9 %collective-permute-start.12 = (bf16[192,1920]{1,0:T(8,128)(2,1)S(1)}, bf16[192,1920]{1,0:T(8,128)(2,1)S(1)}, u32[]{:S(2)}, u32[]{:S(2)}) collective-permute-start(bf16[192,1920]{1,0:T(8,128)(2,1)S(1)} %collective-permute-done.3), channel_id=1, source_target_pairs={{0,4},{1,5},{2,6},{3,7},{4,0},{5,1},{6,2},{7,3},{8,12},{9,13},{10,... | collective-permute-start | bytes 2211848 | tf_op jit(solution)/shard_map/ppermute | solution.py:424
  83.1 27.9 %collective-permute-start.4 = (bf16[192,1920]{1,0:T(8,128)(2,1)S(1)}, bf16[192,1920]{1,0:T(8,128)(2,1)S(1)}, u32[]{:S(2)}, u32[]{:S(2)}) collective-permute-start(bf16[192,1920]{1,0:T(8,128)(2,1)S(1)} %collective-permute-done.3), channel_id=1, source_target_pairs={{0,8},{1,9},{2,10},{3,11},{4,12},{5,13},{6,14},{7,15},{8,16},{9,17... | collective-permute-start | bytes 2211848 | tf_op jit(solution)/shard_map/ppermute | solution.py:424
  110.9 35.1 %collective-permute-start.13 = (bf16[192,1920]{1,0:T(8,128)(2,1)S(1)}, bf16[192,1920]{1,0:T(8,128)(2,1)S(1)}, u32[]{:S(2)}, u32[]{:S(2)}) collective-permute-start(bf16[192,1920]{1,0:T(8,128)(2,1)S(1)} %collective-permute-done.4), channel_id=1, source_target_pairs={{0,4},{1,5},{2,6},{3,7},{4,0},{5,1},{6,2},{7,3},{8,12},{9,13},{10,... | collective-permute-start | bytes 2211848 | tf_op jit(solution)/shard_map/ppermute | solution.py:424
  112.4 30.8 %collective-permute-start.5 = (bf16[192,1920]{1,0:T(8,128)(2,1)S(1)}, bf16[192,1920]{1,0:T(8,128)(2,1)S(1)}, u32[]{:S(2)}, u32[]{:S(2)}) collective-permute-start(bf16[192,1920]{1,0:T(8,128)(2,1)S(1)} %collective-permute-done.4), channel_id=1, source_target_pairs={{0,8},{1,9},{2,10},{3,11},{4,12},{5,13},{6,14},{7,15},{8,16},{9,17... | collective-permute-start | bytes 2211848 | tf_op jit(solution)/shard_map/ppermute | solution.py:424
  143.2 17.2 %collective-permute-start.14 = (bf16[192,1920]{1,0:T(8,128)(2,1)S(1)}, bf16[192,1920]{1,0:T(8,128)(2,1)S(1)}, u32[]{:S(2)}, u32[]{:S(2)}) collective-permute-start(bf16[192,1920]{1,0:T(8,128)(2,1)S(1)} %collective-permute-done.5), channel_id=1, source_target_pairs={{0,4},{1,5},{2,6},{3,7},{4,0},{5,1},{6,2},{7,3},{8,12},{9,13},{10,... | collective-permute-start | bytes 2211848 | tf_op jit(solution)/shard_map/ppermute | solution.py:424
  243.5 243.3 %reduce-scatter.3.cloned.1.call-start = ((), (), s32[]{:S(2)}) async-start(), calls=%async_computation.4 | async-start | bytes 7864320 | tf_op jit(solution)/shard_map/reduce_scatter | solution.py:704
  325.1 112.6 %collective-permute-start.19 = (bf16[2,512,1536]{2,1,0:T(8,128)(2,1)}, bf16[2,512,1536]{2,1,0:T(8,128)(2,1)}, u32[]{:S(2)}, u32[]{:S(2)}) collective-permute-start(bf16[2,512,1536]{2,1,0:T(8,128)(2,1)} %fusion.28), channel_id=1, source_target_pairs={{0,1},{1,0},{2,3},{3,2},{4,5},{5,4},{6,7},{7,6},{8,9},{9,8},{10,11... | collective-permute-start | bytes 9437192 | tf_op jit(solution)/shard_map/ppermute | solution.py:424
  327.1 27.3 %collective-permute-start.42 = (f32[48,128]{1,0:T(8,128)S(1)}, f32[48,128]{1,0:T(8,128)S(1)}, u32[]{:S(2)}, u32[]{:S(2)}) collective-permute-start(f32[48,128]{1,0:T(8,128)S(1)} %pad_bitcast_fusion), channel_id=1, source_target_pairs={{0,4},{1,5},{2,6},{3,7},{4,0},{5,1},{6,2},{7,3},{8,12},{9,13},{10,... | collective-permute-start | bytes 73736 | tf_op jit(solution)/shard_map/ppermute | solution.py:424
  343.5 22.5 %collective-permute-start.31 = (bf16[192,896]{1,0:T(8,128)(2,1)}, bf16[192,896]{1,0:T(8,128)(2,1)}, u32[]{:S(2)}, u32[]{:S(2)}) collective-permute-start(bf16[192,896]{1,0:T(8,128)(2,1)} %get-tuple-element.51), channel_id=1, source_target_pairs={{0,4},{1,5},{2,6},{3,7},{4,0},{5,1},{6,2},{7,3},{8,12},{9,13},{10,... | collective-permute-start | bytes 1032200 | tf_op jit(solution)/shard_map/ppermute | solution.py:424
  360.4 28.6 %collective-permute-start.35 = (bf16[192,896]{1,0:T(8,128)(2,1)}, bf16[192,896]{1,0:T(8,128)(2,1)}, u32[]{:S(2)}, u32[]{:S(2)}) collective-permute-start(bf16[192,896]{1,0:T(8,128)(2,1)} %get-tuple-element.53), channel_id=1, source_target_pairs={{0,4},{1,5},{2,6},{3,7},{4,0},{5,1},{6,2},{7,3},{8,12},{9,13},{10,... | collective-permute-start | bytes 1032200 | tf_op jit(solution)/shard_map/ppermute | solution.py:424
  362.5 16.6 %collective-permute-start.33 = (bf16[192,896]{1,0:T(8,128)(2,1)}, bf16[192,896]{1,0:T(8,128)(2,1)}, u32[]{:S(2)}, u32[]{:S(2)}) collective-permute-start(bf16[192,896]{1,0:T(8,128)(2,1)} %get-tuple-element.54), channel_id=1, source_target_pairs={{0,4},{1,5},{2,6},{3,7},{4,0},{5,1},{6,2},{7,3},{8,12},{9,13},{10,... | collective-permute-start | bytes 1032200 | tf_op jit(solution)/shard_map/ppermute | solution.py:424
  365.7 21.9 %collective-permute-start.21 = (bf16[192,1024]{1,0:T(8,128)(2,1)S(1)}, bf16[192,1024]{1,0:T(8,128)(2,1)}, u32[]{:S(2)}, u32[]{:S(2)}) collective-permute-start(bf16[192,1024]{1,0:T(8,128)(2,1)S(1)} %get-tuple-element.47), channel_id=1, source_target_pairs={{0,4},{1,5},{2,6},{3,7},{4,0},{5,1},{6,2},{7,3},{8,12},{9,13},{10,... | collective-permute-start | bytes 1179656 | tf_op jit(solution)/shard_map/ppermute | solution.py:424
  379.1 23.5 %collective-permute-start.23 = (bf16[192,1024]{1,0:T(8,128)(2,1)S(1)}, bf16[192,1024]{1,0:T(8,128)(2,1)S(1)}, u32[]{:S(2)}, u32[]{:S(2)}) collective-permute-start(bf16[192,1024]{1,0:T(8,128)(2,1)S(1)} %get-tuple-element.50), channel_id=1, source_target_pairs={{0,4},{1,5},{2,6},{3,7},{4,0},{5,1},{6,2},{7,3},{8,12},{9,13},{10,... | collective-permute-start | bytes 1179656 | tf_op jit(solution)/shard_map/ppermute | solution.py:424
  386.1 12.8 %collective-permute-start.34 = (bf16[192,896]{1,0:T(8,128)(2,1)S(1)}, bf16[192,896]{1,0:T(8,128)(2,1)S(1)}, u32[]{:S(2)}, u32[]{:S(2)}) collective-permute-start(bf16[192,896]{1,0:T(8,128)(2,1)S(1)} %fusion.47), channel_id=1, source_target_pairs={{0,8},{1,9},{2,10},{3,11},{4,12},{5,13},{6,14},{7,15},{8,16},{9,17... | collective-permute-start | bytes 1032200 | tf_op jit(solution)/shard_map/ppermute | solution.py:424
  388.8 18.6 %collective-permute-start.22 = (bf16[192,1024]{1,0:T(8,128)(2,1)S(1)}, bf16[192,1024]{1,0:T(8,128)(2,1)S(1)}, u32[]{:S(2)}, u32[]{:S(2)}) collective-permute-start(bf16[192,1024]{1,0:T(8,128)(2,1)S(1)} %fusion.41), channel_id=1, source_target_pairs={{0,8},{1,9},{2,10},{3,11},{4,12},{5,13},{6,14},{7,15},{8,16},{9,17... | collective-permute-start | bytes 1179656 | tf_op jit(solution)/shard_map/ppermute | solution.py:424
  389.0 23.8 %collective-permute-start.37 = (bf16[192,896]{1,0:T(8,128)(2,1)}, bf16[192,896]{1,0:T(8,128)(2,1)}, u32[]{:S(2)}, u32[]{:S(2)}) collective-permute-start(bf16[192,896]{1,0:T(8,128)(2,1)} %get-tuple-element.52), channel_id=1, source_target_pairs={{0,4},{1,5},{2,6},{3,7},{4,0},{5,1},{6,2},{7,3},{8,12},{9,13},{10,... | collective-permute-start | bytes 1032200 | tf_op jit(solution)/shard_map/ppermute | solution.py:424
  398.9 18.1 %collective-permute-start.25 = (bf16[192,1024]{1,0:T(8,128)(2,1)S(1)}, bf16[192,1024]{1,0:T(8,128)(2,1)S(1)}, u32[]{:S(2)}, u32[]{:S(2)}) collective-permute-start(bf16[192,1024]{1,0:T(8,128)(2,1)S(1)} %get-tuple-element.49), channel_id=1, source_target_pairs={{0,4},{1,5},{2,6},{3,7},{4,0},{5,1},{6,2},{7,3},{8,12},{9,13},{10,... | collective-permute-start | bytes 1179656 | tf_op jit(solution)/shard_map/ppermute | solution.py:424
  402.6 13.0 %collective-permute-start.36 = (bf16[192,896]{1,0:T(8,128)(2,1)}, bf16[192,896]{1,0:T(8,128)(2,1)}, u32[]{:S(2)}, u32[]{:S(2)}) collective-permute-start(bf16[192,896]{1,0:T(8,128)(2,1)} %fusion.45), channel_id=1, source_target_pairs={{0,8},{1,9},{2,10},{3,11},{4,12},{5,13},{6,14},{7,15},{8,16},{9,17... | collective-permute-start | bytes 1032200 | tf_op jit(solution)/shard_map/ppermute | solution.py:424
  412.8 14.7 %collective-permute-start.27 = (bf16[192,1024]{1,0:T(8,128)(2,1)S(1)}, bf16[192,1024]{1,0:T(8,128)(2,1)S(1)}, u32[]{:S(2)}, u32[]{:S(2)}) collective-permute-start(bf16[192,1024]{1,0:T(8,128)(2,1)S(1)} %get-tuple-element.48), channel_id=1, source_target_pairs={{0,4},{1,5},{2,6},{3,7},{4,0},{5,1},{6,2},{7,3},{8,12},{9,13},{10,... | collective-permute-start | bytes 1179656 | tf_op jit(solution)/shard_map/ppermute | solution.py:424
  422.1 11.6 %collective-permute-start.40 = (bf16[48,896]{1,0:T(8,128)(2,1)S(1)}, bf16[48,896]{1,0:T(8,128)(2,1)S(1)}, u32[]{:S(2)}, u32[]{:S(2)}) collective-permute-start(bf16[48,896]{1,0:T(8,128)(2,1)S(1)} %get-tuple-element.87), channel_id=1, source_target_pairs={{0,3},{1,0},{2,1},{3,2},{4,7},{5,4},{6,5},{7,6},{8,11},{9,8},{10,9... | collective-permute-start | bytes 258056 | tf_op jit(solution)/shard_map/ppermute | solution.py:424
  433.7 13.9 %collective-permute-start.30 = (bf16[48,1024]{1,0:T(8,128)(2,1)S(1)}, bf16[48,1024]{1,0:T(8,128)(2,1)S(1)}, u32[]{:S(2)}, u32[]{:S(2)}) collective-permute-start(bf16[48,1024]{1,0:T(8,128)(2,1)S(1)} %get-tuple-element.83), channel_id=1, source_target_pairs={{0,3},{1,0},{2,1},{3,2},{4,7},{5,4},{6,5},{7,6},{8,11},{9,8},{10,9... | collective-permute-start | bytes 294920 | tf_op jit(solution)/shard_map/ppermute | solution.py:424
  435.5 12.2 %collective-permute-start.29 = (bf16[48,1024]{1,0:T(8,128)(2,1)S(1)}, bf16[48,1024]{1,0:T(8,128)(2,1)S(1)}, u32[]{:S(2)}, u32[]{:S(2)}) collective-permute-start(bf16[48,1024]{1,0:T(8,128)(2,1)S(1)} %get-tuple-element.84), channel_id=1, source_target_pairs={{0,2},{1,3},{2,0},{3,1},{4,6},{5,7},{6,4},{7,5},{8,10},{9,11},{10,... | collective-permute-start | bytes 294920 | tf_op jit(solution)/shard_map/ppermute | solution.py:424
  446.6 40.2 %collective-permute-start.20 = (bf16[512,1536]{1,0:T(8,128)(2,1)}, bf16[512,1536]{1,0:T(8,128)(2,1)}, u32[]{:S(2)}, u32[]{:S(2)}) collective-permute-start(bf16[512,1536]{1,0:T(8,128)(2,1)} %fusion.33), channel_id=1, source_target_pairs={{0,2},{1,3},{2,0},{3,1},{4,6},{5,7},{6,4},{7,5},{8,10},{9,11},{10,... | collective-permute-start | bytes 4718600 | tf_op jit(solution)/shard_map/ppermute | solution.py:424
  (40 other events, 537.8 us)
Sparse Core Ops, SparseCore 0:
  9.6 56.8 all-gather.4
  69.2 75.9 all-gather.6
  146.9 44.4 all-gather.8
  243.6 69.8 reduce-scatter.4
  320.3 62.6 reduce-scatter.2
